TPU v7x, 128 devices: a whole 4x4x4 slice. The times are simulated.
128 devices in a mesh: gx: 16 (over y, z), gy: 8 (over x, core).
Axes of the slice: x: 4, y: 4, z: 4, core: 2. Of those that a mesh axis runs over, the one named last changes fastest.
Arguments:
- stream: bfloat16 [256, 18432], P(('gx', 'gy')), may hold values from -6 to 6
- norm_gain: float32 [18432], replicated, may hold values from 0.1 to 1.9
- w_gate: bfloat16 [18432, 36864], P('gx', 'gy'), may hold values from -0.046875 to 0.046875
- w_up: bfloat16 [18432, 36864], P('gx', 'gy'), may hold values from -0.046875 to 0.046875
- w_query: bfloat16 [18432, 6144], P('gx', 'gy'), may hold values from -0.046875 to 0.046875
- w_keyval: bfloat16 [18432, 512], P('gx', 'gy'), may hold values from -0.046875 to 0.046875
- k_cache: bfloat16 [256, 512, 256], P(('gx', 'gy')), may hold values from -200 to 200
- v_cache: bfloat16 [256, 512, 256], P(('gx', 'gy')), may hold values from -6 to 6
- lengths: int32 [256], P(('gx', 'gy')), may hold values from 1 to 512, 65536 in all
Outputs:
- hidden: bfloat16 [256, 36864], P('gx', 'gy')
- context: bfloat16 [256, 6144], P(('gx', 'gy'))
Inputs may be any that keep to these rules, and one draw needn't show every extreme that they name: `lengths`: some row has 512 filled slots.
All inputs are finite; a program needn't handle non-finite values. No bound on the sum of `lengths` on one device may be relied on, other than what follows from the above.
Results may differ from a plain program's by a relative error of at most 0.017.
The roundings to bfloat16 on the way count: a program that leaves them out, or rounds other values in their place, can miss the bound.
Values may be sent and summed in bfloat16 or wider, within the bound.
A program may use at most 128 MiB of HBM per device.

v0:
```python
import jax
import jax.numpy as jnp
from jax import lax
from jax.sharding import PartitionSpec as P

HEADS = 24
DH = 256


def body(stream, norm_gain, w_gate, w_up, w_query, w_keyval, k_cache, v_cache, lengths):
    values = stream.astype(jnp.float32)
    mean = jnp.mean(values, axis=1, keepdims=True)
    centred = values - mean
    variance = jnp.mean(centred * centred, axis=1, keepdims=True)
    normed = (centred / jnp.sqrt(variance + 1e-05) * norm_gain[None, :]).astype(jnp.bfloat16)
    block_width = w_gate.shape[0]
    whole = lax.all_gather(normed, ("gx", "gy"), axis=0, tiled=True)
    offset = lax.axis_index("gx") * block_width
    rows_in = lax.dynamic_slice_in_dim(whole, offset, block_width, 1)
    ff_local = w_gate.shape[1]
    block = rows_in
    attn_part = lax.psum_scatter(
        jnp.concatenate(
            [
                jnp.dot(block, w_query, preferred_element_type=jnp.float32),
                jnp.dot(block, w_keyval, preferred_element_type=jnp.float32),
            ],
            axis=1,
        ),
        "gx",
        scatter_dimension=0,
        tiled=True,
    )
    block = rows_in
    ffn_part = lax.psum_scatter(
        jnp.concatenate(
            [
                jnp.dot(block, w_gate, preferred_element_type=jnp.float32),
                jnp.dot(block, w_up, preferred_element_type=jnp.float32),
            ],
            axis=1,
        ),
        "gx",
        scatter_dimension=0,
        tiled=True,
    )
    hidden = (jax.nn.silu(ffn_part[:, :ff_local]) * ffn_part[:, ff_local:]).astype(jnp.bfloat16)
    projected = attn_part.astype(jnp.bfloat16)
    row_major = lax.all_to_all(projected, "gy", split_axis=0, concat_axis=1, tiled=True)
    groups = lax.axis_size("gy")
    query_cols = w_query.shape[1]
    keyval_cols = w_keyval.shape[1]
    rows = row_major.shape[0]
    pieces = row_major.reshape(rows, groups, query_cols + keyval_cols)
    query = pieces[:, :, :query_cols].reshape(rows, HEADS, DH)
    keyval = pieces[:, :, query_cols:].reshape(rows, groups * keyval_cols)
    new_key = keyval[:, :DH]
    new_value = keyval[:, DH:]
    scale = DH ** (-0.5)
    scores = jnp.einsum("bhd,bld->bhl", query, k_cache, preferred_element_type=jnp.float32) * scale
    score_new = jnp.einsum("bhd,bd->bh", query, new_key, preferred_element_type=jnp.float32) * scale
    mask = (jnp.arange(k_cache.shape[1], dtype=jnp.int32)[None, :] < lengths[:, None])[:, None, :]
    top = jnp.maximum(jnp.max(jnp.where(mask, scores, -1e30), axis=2), score_new)
    exponent = jnp.where(mask, jnp.exp(scores - top[:, :, None]), 0.0)
    exponent_new = jnp.exp(score_new - top)
    total = jnp.sum(exponent, axis=2) + exponent_new
    weights = (exponent / total[:, :, None]).astype(jnp.bfloat16)
    weights_new = (exponent_new / total).astype(jnp.bfloat16)
    context = jnp.einsum("bhl,bld->bhd", weights, v_cache, preferred_element_type=jnp.float32)
    context = (
        context
        + weights_new.astype(jnp.float32)[:, :, None] * new_value.astype(jnp.float32)[:, None, :]
    )
    return (hidden, context.reshape(rows, HEADS * DH).astype(jnp.bfloat16))


def solution(mesh):
    return jax.shard_map(
        body,
        mesh=mesh,
        in_specs=(
            P(("gx", "gy"), None),
            P(),
            P("gx", "gy"),
            P("gx", "gy"),
            P("gx", "gy"),
            P("gx", "gy"),
            P(("gx", "gy"), None, None),
            P(("gx", "gy"), None, None),
            P(("gx", "gy")),
        ),
        out_specs=(P("gx", "gy"), P(("gx", "gy"), None)),
        check_vma=False,
    )
```

profile of v0, /device:TPU:1, one launch (start us, length us, event | category | flops | bytes accessed | tf_op | source)
XLA Modules:
  0.0 243.4 jit_solution(10122546581420066397)
XLA Ops:
  7.2 0.0 copy-start
  7.2 0.0 all-gather.3.cloned.1.call-start
  7.2 1.3 convert_reduce_fusion
  8.5 1.2 fusion.15
  9.7 1.7 fusion.17
  11.5 0.0 all-gather.3.cloned.1.call-update
  11.5 0.0 reduce-scatter.2.cloned.1.call-start
  11.5 74.1 %all-gather.3.cloned.1.call-done = bf16[128,2,18432]{2,1,0:T(2,128)(2,1)} async-done(((bf16[1,2,18432]{2,1,0:T(2,128)(2,1)}), bf16[128,2,18432]{2,1,0:T(2,128)(2,1)}) %all-gather.3.cloned.1.call-update) | async-done | bytes 9437200 | tf_op jit(solution)/shard_map/all_gather | solution.py:17
  85.6 13.8 %reshape.54 = bf16[256,18432]{1,0:T(8,128)(2,1)} reshape(bf16[128,2,18432]{2,1,0:T(2,128)(2,1)} %all-gather.3.cloned.1.call-done) | data formatting | bytes 18874368
  99.4 6.1 %fusion.6 = f32[256,4608]{1,0:T(8,128)S(1)} fusion(bf16[1152,4608]{1,0:T(8,128)(2,1)} %param.12, bf16[256,18432]{1,0:T(8,128)(2,1)} %reshape.54, s32[]{:T(128)S(6)} %select_n.10), kind=kOutput, calls=%fused_computation.10 | convolution fusion | flops 2717908992 | bytes 15925252 | tf_op jit(solution)/shard_map/dot_general | solution.py:39
  105.5 9.6 %fusion.8 = f32[256,4608]{1,0:T(8,128)} fusion(bf16[1152,4608]{1,0:T(8,128)(2,1)} %param.11, bf16[256,18432]{1,0:T(8,128)(2,1)} %reshape.54, s32[]{:T(128)S(6)} %select_n.10), kind=kOutput, calls=%fused_computation.12 | convolution fusion | flops 2717908992 | bytes 15925252 | tf_op jit(solution)/shard_map/dot_general | solution.py:38
  115.1 6.8 %pad_maximum_fusion = f32[256,9216]{1,0:T(8,128)} fusion(f32[256,4608]{1,0:T(8,128)S(1)} %fusion.6, f32[256,4608]{1,0:T(8,128)} %fusion.8), kind=kLoop, calls=%fused_computation | loop fusion | flops 2359296 | bytes 18874368 | tf_op jit(solution)/shard_map/concatenate | solution.py:36
  121.9 0.0 reduce-scatter.2.cloned.1.call-update
  121.9 0.6 copy-done.4
  122.5 0.6 dynamic-slice
  123.8 1.4 fusion.2
  125.1 0.0 copy-done
  125.1 1.7 fusion.4
  126.9 0.1 pad_maximum_fusion.1
  127.0 82.0 %all-reduce.2 = bf16[256,832]{1,0:T(8,128)(2,1)} all-reduce(f32[256,832]{1,0:T(8,128)S(1)} %pad_maximum_fusion.1), channel_id=3, replica_groups=mesh['gx'=16,'gy'=8] {'gx'}, use_global_device_ids=true, to_apply=%region_3.0.clone | all-reduce | flops 212992 | bytes 1277952
  208.9 0.8 dynamic-slice_convert_fusion
  209.7 0.6 all_to_all.12
  210.3 17.0 %all-to-all-start = ((bf16[8,2,832]{2,1,0:T(2,128)(2,1)}), bf16[8,2,832]{2,1,0:T(2,128)(2,1)S(1)}, u32[]{:S(2)}, u32[]{:S(2)}) async-start(bf16[8,2,832]{2,1,0:T(2,128)(2,1)} %all_to_all.12), calls=%async_computation.1 | async-start | bytes 57344 | tf_op jit(solution)/shard_map/all_to_all | solution.py:49
  227.3 0.1 iota_compare_fusion
  227.4 4.6 %all-to-all-done = bf16[8,2,832]{2,1,0:T(2,128)(2,1)S(1)} async-done(((bf16[8,2,832]{2,1,0:T(2,128)(2,1)}), bf16[8,2,832]{2,1,0:T(2,128)(2,1)S(1)}, u32[]{:S(2)}, u32[]{:S(2)}) %all-to-all-start) | async-done | bytes 26656 | tf_op jit(solution)/shard_map/all_to_all | solution.py:49
  232.1 0.1 reshape.52
  232.2 0.1 fusion.22
  232.3 0.3 select_reduce_fusion
  232.6 0.2 fusion.16
  232.8 1.3 fusion.1
  234.1 0.6 copy.21
  234.8 1.8 fusion.10
  (18 shorter events, 0.1 us)
Async XLA Ops:
  7.2 118.0 %copy-start = (bf16[1152,768]{1,0:T(8,128)(2,1)S(1)}, bf16[1152,768]{1,0:T(8,128)(2,1)}, u32[]{:S(2)}) copy-start(bf16[1152,768]{1,0:T(8,128)(2,1)} %param.13) | copy-start | bytes 5308420
  7.2 78.4 %all-gather.3.cloned.1.call-start = ((), (), s32[]{:S(2)}) async-start(), calls=%async_computation.3 | async-start | bytes 9510912 | tf_op jit(solution)/shard_map/all_gather | solution.py:17
  11.5 223.3 %reduce-scatter.2.cloned.1.call-start = ((), (), s32[]{:S(2)}) async-start(), calls=%async_computation.2 | async-start | bytes 10027008 | tf_op jit(solution)/shard_map/reduce_scatter | solution.py:35
  121.9 0.7 copy-start.4
  121.9 1.9 copy-start.2
  121.9 105.4 %copy-start.3 = (s32[2]{0:T(128)S(1)}, s32[2]{0:T(128)}, u32[]{:S(2)}) copy-start(s32[2]{0:T(128)} %param.17) | copy-start | bytes 28
  121.9 110.4 %copy-start.1 = (bf16[2,512,256]{2,1,0:T(8,128)(2,1)S(1)}, bf16[2,512,256]{2,1,0:T(8,128)(2,1)}, u32[]{:S(2)}) copy-start(bf16[2,512,256]{2,1,0:T(8,128)(2,1)} %param.15) | copy-start | bytes 1572868
  210.3 21.7 %all-to-all-start = ((bf16[8,2,832]{2,1,0:T(2,128)(2,1)}), bf16[8,2,832]{2,1,0:T(2,128)(2,1)S(1)}, u32[]{:S(2)}, u32[]{:S(2)}) async-start(bf16[8,2,832]{2,1,0:T(2,128)(2,1)} %all_to_all.12), calls=%async_computation.1 | async-start | bytes 57344 | tf_op jit(solution)/shard_map/all_to_all | solution.py:49
Sparse Core Ops, SparseCore 0:
  11.6 73.9 all-gather.2
  122.0 93.7 reduce-scatter.1
where the time goes:
time: 244 us; the launch traced here: 243 us
  blocking collectives  82 us (34%)
  waiting for transfers between devices  78.7 us (32%)
  matrix products  20.5 us (8%)
  local copies, waits for them, and re-layouts  17.2 us (7%)
  starting transfers between devices  17.1 us (7%)
  between operations  14.8 us (6%)
  other arithmetic  13.2 us (5%)
    unnamed x1, blocking collectives  82 us
    all_gather x1, waiting for transfers between devices, body(): whole = lax.all_gather(normed, ('gx', 'gy'), axis=0, tiled=True)  74.1 us
    all_to_all x1, starting transfers between devices, body(): lax.all_to_all(projected, 'gy', split_axis=0, concat_axis=1, tiled=True)  17 us
    unnamed x13, local copies, waits for them, and re-layouts  15.7 us
    dot_general x1, matrix products, body(): jnp.dot(block, w_gate, preferred_element_type=jnp.float32)  9.6 us
    concatenate x1, other arithmetic, body(): jnp.concatenate([jnp.dot(block, w_gate, preferred_element_type=jnp.float3...  6.8 us
    dot_general x1, matrix products, body(): jnp.dot(block, w_up, preferred_element_type=jnp.float32)  6.06 us
  transfers between devices with their start and end apart: 3, of which 2 were waited for; matrix products, arithmetic and copies ran while one was open for 3% of the time, Pallas kernels for 0%

commit v1 on v0

v1 whole, which is shorter than its diff:
```python
import jax
import jax.numpy as jnp
from jax import lax
from jax.experimental import pallas as pl
from jax.experimental.pallas import tpu as pltpu
from jax.sharding import PartitionSpec as P

HEADS = 24
DH = 256
D = 18432
K = 1152
FF = 4608
T = 12
W = FF // T
MESH = pl.DeviceIdType.MESH
F32 = jnp.float32
BF16 = jnp.bfloat16


def f32(v):
    return v.astype(F32)


def chunk(ref, axis, i):
    return ref.at[i] if axis == "y" else ref.at[:, i]


class Place:
    def __init__(self):
        gx, self.gy = lax.axis_index("gx"), lax.axis_index("gy")
        self.y, self.z = lax.div(gx, 4), lax.rem(gx, 4)
        self.x, self.c = lax.div(self.gy, 2), lax.rem(self.gy, 2)
        self.gx = gx

    def at(self, axis, k):
        return lax.rem((self.y if axis == "y" else self.z) + (k % 4), 4)

    def dev(self, axis, k):
        if axis == "y":
            return (self.at("y", k) * 4 + self.z, self.gy)
        return (self.y * 4 + self.at("z", k), self.gy)


class Stream:
    def __init__(self, here, first, s, p, far1, rel1, near1, mid, far2, rel2, near2, ss, rs):
        self.here, self.s, self.ss, self.rs = here, s, ss, rs
        self.ax = (first, "z" if first == "y" else "y")
        self.p, self.mid = p, mid
        self.far, self.rel, self.near = (far1, far2), (rel1, rel2), (near1, near2)

    def own(self, ph, k):
        at = self.here.at(self.ax[ph], k)
        return chunk(self.p, self.ax[0], at) if ph == 0 else self.mid.at[at]

    def copy(self, ph, i):
        s = self.s
        src, dst, k = (
            (self.own(ph, 2), self.far[ph], s),
            (self.own(ph, -s), self.near[ph], -s),
            (self.far[ph], self.rel[ph], s),
        )[i]
        return pltpu.make_async_remote_copy(
            src, dst, self.ss.at[ph * 3 + i], self.rs.at[ph * 3 + i],
            device_id=self.here.dev(self.ax[ph], k), device_id_type=MESH,
        )

    def start(self, ph):
        self.copy(ph, 0).start()
        self.copy(ph, 1).start()

    def relay(self, ph):
        self.copy(ph, 0).wait_recv()
        ref = self.far[ph]
        ref[...] = (f32(ref[...]) + f32(self.own(ph, self.s)[...])).astype(ref.dtype)
        self.copy(ph, 2).start()

    def total(self, ph):
        self.copy(ph, 1).wait_recv()
        self.copy(ph, 2).wait_recv()
        return f32(self.own(ph, 0)[...]) + f32(self.rel[ph][...]) + f32(self.near[ph][...])

    def turn(self):
        self.mid[...] = self.total(0).astype(self.mid.dtype)
        self.start(1)

    def drain(self):
        for ph in (0, 1):
            for i in range(3):
                self.copy(ph, i).wait_send()


def kernel(
    stream_h, gain_h, wg_h, wu_h, wq_h, wkv_h,
    hidden, qkv,
    stream, gain, wg, wu, wq, wkv, load_sem, wsem,
    nsend, ybuf, zbuf, a32, xr, perm, xs,
    d_ss, d_rs,
    fp, ff1, fr1, fn1, fm, ff2, fr2, fn2, f_ss, f_rs,
    qp, qf1, qr1, qn1, qm, qf2, qr2, qn2,
    vp, vf1, vr1, vn1, vm, vf2, vr2, vn2, a_ss, a_rs,
    qs, g_ss, g_rs,
):
    h = Place()
    loads = [
        pltpu.make_async_copy(src, dst, load_sem.at[i])
        for i, (src, dst) in enumerate([(stream_h, stream), (gain_h, gain), (wq_h, wq), (wkv_h, wkv)])
    ]
    for c in loads:
        c.start()

    def wload(t):
        cols = pl.ds(pl.multiple_of(t * W, 128), W)
        return (
            pltpu.make_async_copy(wg_h.at[:, cols], wg.at[t], wsem.at[t, 0]),
            pltpu.make_async_copy(wu_h.at[:, cols], wu.at[t], wsem.at[t, 1]),
        )

    @pl.loop(0, T)
    def _(t):
        for c in wload(t):
            c.start()

    bar = pltpu.get_barrier_semaphore()
    for ax in "yz":
        for k in (1, 2, 3):
            pl.semaphore_signal(bar, inc=1, device_id=h.dev(ax, k), device_id_type=MESH)
    for k in range(1, 8):
        pl.semaphore_signal(bar, inc=1, device_id=(h.gx, lax.rem(h.gy + k, 8)), device_id_type=MESH)

    i = lax.broadcasted_iota(jnp.int32, (256, 256), 0)
    j = lax.broadcasted_iota(jnp.int32, (256, 256), 1)
    want = ((i >> 1) & 7) * 32 + (i >> 4) * 2 + (i & 1)
    perm[...] = jnp.where(want == j, 1.0, 0.0).astype(BF16)
    vp[...] = jnp.zeros_like(vp)

    loads[0].wait()
    loads[1].wait()
    total = jnp.zeros((2, K), F32)
    for q in range(16):
        total += f32(stream[:, q * K:(q + 1) * K])
    mean = jnp.sum(total, axis=1, keepdims=True) * (1.0 / D)
    total = jnp.zeros((2, K), F32)
    for q in range(16):
        v = f32(stream[:, q * K:(q + 1) * K]) - mean
        total += v * v
    root = jnp.sqrt(jnp.sum(total, axis=1, keepdims=True) * (1.0 / D) + 1e-05)
    for q in range(16):
        v = (f32(stream[:, q * K:(q + 1) * K]) - mean) / root * gain[:, q * K:(q + 1) * K]
        nsend[q // 4, :, (q % 4) * K:(q % 4 + 1) * K] = v.astype(BF16)

    pl.semaphore_wait(bar, 13)

    first = [
        pltpu.make_async_remote_copy(
            nsend.at[h.at("y", k)], ybuf.at[h.y], d_ss.at[k], d_rs.at[k],
            device_id=h.dev("y", k), device_id_type=MESH)
        for k in (2, 1, 3)
    ]
    for c in first:
        c.start()
    ybuf[h.y] = nsend[h.y]
    for c in first:
        c.wait_recv()

    def zcols(zd):
        return pl.ds(pl.multiple_of(zd * K, 128), K)

    second = [
        pltpu.make_async_remote_copy(
            ybuf.at[:, :, zcols(h.at("z", k))], zbuf.at[h.z], d_ss.at[3 + k], d_rs.at[3 + k],
            device_id=h.dev("z", k), device_id_type=MESH)
        for k in (2, 1, 3)
    ]
    for c in second:
        c.start()
    zbuf[h.z] = ybuf[:, :, zcols(h.z)]
    for c in second:
        c.wait_recv()
    for y in range(4):
        for z in range(4):
            r = (y * 4 + z) * 2
            a32[r:r + 2, :] = f32(zbuf[z, y])
    xr[h.gy] = a32[...].astype(BF16)

    def to_x(k):
        return pltpu.make_async_remote_copy(
            xr.at[h.gy], xr.at[h.gy], d_ss.at[7 + k], d_rs.at[7 + k],
            device_id=(h.gx, lax.rem(h.gy + 2 * k, 8)), device_id_type=MESH)

    def to_partner(k):
        g = lax.rem(h.gy + 8 - 2 * k, 8)
        return pltpu.make_async_remote_copy(
            xr.at[g], xr.at[g], d_ss.at[11 + k], d_rs.at[11 + k],
            device_id=(h.gx, h.x * 2 + 1 - h.c), device_id_type=MESH)

    third = [to_x(k) for k in (2, 1, 3)]
    for c in third:
        c.start()
    fourth = [to_partner(k) for k in range(4)]
    fourth[0].start()
    for k in (1, 3, 2):
        to_x(k).wait_recv()
        fourth[k].start()
    for c in fourth:
        c.wait_recv()
    for n in range(3):
        cols = slice(n * 384, (n + 1) * 384)
        xs[:, cols] = jnp.dot(
            perm[...], xr[:, :, cols].reshape(256, 384), preferred_element_type=F32
        ).astype(BF16)
    for c in first + second + third + fourth:
        c.wait_send()

    att = [
        Stream(h, first, s, qp.at[n], qf1.at[n], qr1.at[n], qn1.at[n], qm.at[n], qf2.at[n], qr2.at[n], qn2.at[n],
               a_ss.at[n], a_rs.at[n])
        for n, (first, s) in enumerate([("y", -1), ("z", 1), ("y", 1)])
    ]
    att.append(Stream(h, "z", -1, vp, vf1, vr1, vn1, vm, vf2, vr2, vn2, a_ss.at[3], a_rs.at[3]))

    def ffn(t, n, order):
        return Stream(h, order, -1 if n == 0 else 1, fp.at[t, n], ff1.at[t, n], fr1.at[t, n], fn1.at[t, n],
                      fm.at[t, n], ff2.at[t, n], fr2.at[t, n], fn2.at[t, n], f_ss.at[t, n], f_rs.at[t, n])

    def pair(i, do):
        for t, order in ((2 * i, "y"), (2 * i + 1, "z")):
            do(t, [ffn(t, n, order) for n in (0, 1)])

    loads[2].wait()
    loads[3].wait()
    for n in range(3):
        qp[n] = jnp.dot(xs[...], wq[:, n * DH:(n + 1) * DH], preferred_element_type=F32).reshape(4, 4, 16, DH)
        att[n].start(0)
    vp[:, :, :, 0:64] = jnp.dot(xs[...], wkv[...], preferred_element_type=F32).reshape(4, 4, 16, 64)
    att[3].start(0)

    def compute(t, streams):
        for c in wload(t):
            c.wait()
        for n, w in ((0, wg), (1, wu)):
            fp[t, n] = jnp.dot(xs[...], w[t], preferred_element_type=F32).astype(BF16).reshape(4, 4, 16, W)
            streams[n].start(0)

    def computes(lo, hi):
        @pl.loop(lo, hi)
        def _(i):
            pair(i, compute)

    computes(0, 2)
    for s in att:
        s.relay(0)
    computes(2, 3)
    for s in att:
        s.turn()
    computes(3, 4)
    for s in att:
        s.relay(1)
    computes(4, T // 2)

    @pl.loop(0, T // 2)
    def _(i):
        pair(i, lambda t, ss: [s.relay(0) for s in ss])

    for n, s in enumerate(att):
        val = s.total(1)
        for g in range(8):
            qs[g, :, n * DH:n * DH + val.shape[1]] = val[2 * g:2 * g + 2, :].astype(BF16)
    give = [
        pltpu.make_async_remote_copy(
            qs.at[lax.rem(h.gy + k, 8)], qkv.at[h.gy], g_ss.at[k], g_rs.at[k],
            device_id=(h.gx, lax.rem(h.gy + k, 8)), device_id_type=MESH)
        for k in range(1, 8)
    ]
    for c in give:
        c.start()
    qkv[h.gy] = qs[h.gy]

    @pl.loop(0, T // 2)
    def _(i):
        pair(i, lambda t, ss: [s.turn() for s in ss])

    @pl.loop(0, T // 2)
    def _(i):
        pair(i, lambda t, ss: [s.relay(1) for s in ss])

    def finish(t, ss):
        gate, up = ss[0].total(1), ss[1].total(1)
        cols = pl.ds(pl.multiple_of(t * W, 128), W)
        hidden[:, cols] = (gate / (1.0 + jnp.exp(-gate)) * up).astype(BF16)

    @pl.loop(0, T // 2)
    def _(i):
        pair(i, finish)

    for c in give:
        c.wait()
    for s in att:
        s.drain()

    @pl.loop(0, T // 2)
    def _(i):
        pair(i, lambda t, ss: [s.drain() for s in ss])


def fused(stream, gain, w_gate, w_up, w_query, w_keyval):
    vm, dma = pltpu.VMEM, pltpu.SemaphoreType.DMA

    def rs(lead, wide, kind):
        return [
            vm(lead + (4, 4, 16, wide), kind),
            *[vm(lead + (4, 16, wide), kind)] * 3,
            vm(lead + (4, 16, wide), kind),
            *[vm(lead + (16, wide), kind)] * 3,
        ]

    return pl.pallas_call(
        kernel,
        out_shape=(
            jax.ShapeDtypeStruct((16, FF), BF16),
            jax.ShapeDtypeStruct((8, 2, 896), BF16),
        ),
        in_specs=[pl.BlockSpec(memory_space=pl.ANY)] * 6,
        out_specs=[pl.BlockSpec(memory_space=pltpu.VMEM)] * 2,
        scratch_shapes=[
            vm((2, D), BF16), vm((1, D), F32), vm((T, K, W), BF16), vm((T, K, W), BF16),
            vm((K, 768), BF16), vm((K, 64), BF16), dma((4,)), dma((T, 2)),
            vm((4, 2, 4 * K), BF16), vm((4, 2, 4 * K), BF16), vm((4, 4, 2, K), BF16), vm((32, K), F32),
            vm((8, 32, K), BF16), vm((256, 256), BF16), vm((256, K), BF16),
            dma((15,)), dma((15,)),
            *rs((T, 2), W, BF16), dma((T, 2, 6)), dma((T, 2, 6)),
            *rs((3,), DH, F32),
            *rs((), 128, F32), dma((4, 6)), dma((4, 6)),
            vm((8, 2, 896), BF16), dma((8,)), dma((8,)),
        ],
        compiler_params=pltpu.CompilerParams(
            collective_id=0, has_side_effects=True, vmem_limit_bytes=62 * 2**20
        ),
    )(stream, gain, w_gate, w_up, w_query, w_keyval)


def body(stream, norm_gain, w_gate, w_up, w_query, w_keyval, k_cache, v_cache, lengths):
    hidden, pieces = fused(stream, norm_gain.reshape(1, D), w_gate, w_up, w_query, w_keyval)
    rows = 2
    pieces = jnp.swapaxes(pieces, 0, 1)
    query = pieces[:, :, :768].reshape(rows, HEADS, DH)
    keyval = pieces[:, :, 768:832].reshape(rows, 512)
    new_key = keyval[:, :DH]
    new_value = keyval[:, DH:]
    scale = DH ** (-0.5)
    scores = jnp.einsum("bhd,bld->bhl", query, k_cache, preferred_element_type=F32) * scale
    score_new = jnp.einsum("bhd,bd->bh", query, new_key, preferred_element_type=F32) * scale
    mask = (jnp.arange(k_cache.shape[1], dtype=jnp.int32)[None, :] < lengths[:, None])[:, None, :]
    top = jnp.maximum(jnp.max(jnp.where(mask, scores, -1e30), axis=2), score_new)
    exponent = jnp.where(mask, jnp.exp(scores - top[:, :, None]), 0.0)
    exponent_new = jnp.exp(score_new - top)
    total = jnp.sum(exponent, axis=2) + exponent_new
    weights = (exponent / total[:, :, None]).astype(BF16)
    weights_new = (exponent_new / total).astype(BF16)
    context = jnp.einsum("bhl,bld->bhd", weights, v_cache, preferred_element_type=F32)
    context = context + f32(weights_new)[:, :, None] * f32(new_value)[:, None, :]
    return (hidden, context.reshape(rows, HEADS * DH).astype(BF16))


def solution(mesh):
    return jax.shard_map(
        body,
        mesh=mesh,
        in_specs=(
            P(("gx", "gy"), None),
            P(),
            P("gx", "gy"),
            P("gx", "gy"),
            P("gx", "gy"),
            P("gx", "gy"),
            P(("gx", "gy"), None, None),
            P(("gx", "gy"), None, None),
            P(("gx", "gy")),
        ),
        out_specs=(P("gx", "gy"), P(("gx", "gy"), None)),
        check_vma=False,
    )
```

time: 244 us -> 68.8 us (0.28)
  blocking collectives: 82 us -> 0 us
  waiting for transfers between devices: 78.7 us -> 0 us
  Pallas kernels: 0 us -> 60.2 us
  matrix products: 20.5 us -> 0.7 us
  starting transfers between devices: 17.1 us -> 0 us
  between operations: 14.8 us -> 0.68 us
  other arithmetic: 13.2 us -> 0.28 us
  local copies, waits for them, and re-layouts: 17.2 us -> 5.63 us
    unnamed x1 -> x0, blocking collectives: 82 us -> none
    all_gather x1 -> x0, waiting for transfers between devices: 74.1 us -> none  [body(): whole = lax.all_gather(normed, ('gx', 'gy'), axis=0, tiled=True)]
    pallas_call x0 -> x1, Pallas kernels: none -> 60.2 us  [fused(): pl.pallas_call(kernel, out_shape=(jax.ShapeDtypeStruct((16, FF), BF16), j...]
    dot_general x7 -> x3, matrix products: 20.5 us -> 0.7 us  [the longest x1 0.33 us: body(): jnp.einsum('bhd,bld->bhl', query, k_cache, preferred_element_type=F32)]
    all_to_all x1 -> x0, starting transfers between devices: 17 us -> none  [body(): lax.all_to_all(projected, 'gy', split_axis=0, concat_axis=1, tiled=True)]
    unnamed x13 -> x9, local copies, waits for them, and re-layouts: 15.7 us -> 4.08 us
    concatenate x2 -> x0, other arithmetic: 6.86 us -> none  [the longest x1 6.8 us: body(): jnp.concatenate([jnp.dot(block, w_gate, preferred_element_type=jnp.float3...]
    all_to_all x1 -> x0, waiting for transfers between devices: 4.63 us -> none  [body(): lax.all_to_all(projected, 'gy', split_axis=0, concat_axis=1, tiled=True)]
  transfers between devices with their start and end apart: 3 -> 0, of which waited for: 2 -> 0; matrix products, arithmetic and copies ran while one was open for 3% -> 0% of each run, Pallas kernels for 0% -> 0%
where the time goes in v1:
time: 68.8 us; the launch traced here: 67.5 us
  Pallas kernels  60.2 us (88%)
  local copies, waits for them, and re-layouts  5.63 us (8%)
  matrix products  0.7 us (1%)
    pallas_call x1, Pallas kernels, fused(): pl.pallas_call(kernel, out_shape=(jax.ShapeDtypeStruct((16, FF), BF16), j...  60.2 us
    unnamed x9, local copies, waits for them, and re-layouts  4.08 us

profile of v1, /device:TPU:1, one launch (start us, length us, event | category | flops | bytes accessed | tf_op | source)
XLA Modules:
  0.0 67.5 jit_solution(10935217026141905474)
XLA Ops:
  0.6 0.0 copy-start
  0.6 1.8 %copy.12.wkv_h = bf16[1152,64]{1,0:T(8,128)(2,1)} copy(bf16[1152,64]{0,1:T(8,128)(2,1)} %param.14) | data formatting | bytes 294912 | tf_op args[5]
  2.5 0.0 copy-start.1
  2.5 0.0 copy-start.2
  2.5 60.2 %shard_map.104 = (bf16[16,4608]{1,0:T(8,128)(2,1)}, bf16[8,2,896]{2,1,0:T(2,128)(2,1)}) custom-call(bf16[2,18432]{1,0:T(2,128)(2,1)} %stream_h.1, f32[1,18432]{1,0:T(1,128)} %bitcast.13, bf16[1152,4608]{1,0:T(8,128)(2,1)} %wg_h.1, bf16[1152,4608]{1,0:T(8,128)(2,1)} %wu_h.1, bf16[1152,768]{1,0:T(8,128)(2,1)} %wq_h.1, bf16[1152,64]{1,0:T(8,128)(2,1)} %copy.12.wkv_h), custom_call_target="tpu_custom_call" | custom-call | tf_op jit(solution)/shard_map/pallas_call | solution.py:316
  62.7 0.8 %slice.16 = bf16[2,8,768]{2,0,1:T(2,128)(2,1)S(1)} slice(bf16[2,8,896]{2,0,1:T(2,128)(2,1)} %bitcast.14), slice={[0:2], [0:8], [0:768]} | slice | bytes 49152 | tf_op jit(solution)/shard_map/slice | solution.py:345
  63.5 0.7 %slice.17 = bf16[2,8,64]{2,0,1:T(2,128)(2,1)S(1)} slice(bf16[2,8,896]{2,0,1:T(2,128)(2,1)} %bitcast.15), slice={[0:2], [0:8], [768:832]} | slice | bytes 4096 | tf_op jit(solution)/shard_map/slice | solution.py:346
  64.2 0.1 reshape.38
  64.3 0.1 fusion.7
  64.4 0.0 copy-done.1
  64.4 0.1 iota_compare_fusion
  64.5 0.0 copy-done
  64.5 0.3 select_reduce_fusion
  64.8 0.2 fusion.2
  65.0 0.0 copy-done.2
  65.0 0.2 fusion.1
  65.3 0.6 copy.17
  65.9 1.6 %copy.21 = bf16[16,4608]{1,0:T(8,128)(2,1)} copy(bf16[16,4608]{1,0:T(8,128)(2,1)} %get-tuple-element.14) | data formatting | bytes 294912
  (6 shorter events, 0.1 us)
Async XLA Ops:
  0.6 63.9 %copy-start = (bf16[2,512,256]{2,1,0:T(8,128)(2,1)S(1)}, bf16[2,512,256]{2,1,0:T(8,128)(2,1)}, u32[]{:S(2)}) copy-start(bf16[2,512,256]{2,1,0:T(8,128)(2,1)} %param.15) | copy-start | bytes 1572868
  2.5 61.9 %copy-start.1 = (s32[2]{0:T(128)S(1)}, s32[2]{0:T(128)}, u32[]{:S(2)}) copy-start(s32[2]{0:T(128)} %param.17) | copy-start | bytes 28
  2.5 62.5 %copy-start.2 = (bf16[2,512,256]{2,1,0:T(8,128)(2,1)S(1)}, bf16[2,512,256]{2,1,0:T(8,128)(2,1)}, u32[]{:S(2)}) copy-start(bf16[2,512,256]{2,1,0:T(8,128)(2,1)} %param.16) | copy-start | bytes 1572868

commit v2 on v1

v2 whole, which is shorter than its diff:
```python
import functools

import jax
import jax.numpy as jnp
from jax import lax
from jax.experimental import pallas as pl
from jax.experimental.pallas import tpu as pltpu
from jax.sharding import PartitionSpec as P

HEADS = 24
DH = 256
D = 18432
K = 1152
FF = 4608
T = 12
DIRECT = 4
CACHE = 512
W = FF // T
MESH = pl.DeviceIdType.MESH
F32 = jnp.float32
BF16 = jnp.bfloat16


def f32(v):
    return v.astype(F32)


def chunk(ref, axis, i):
    return ref.at[i] if axis == "y" else ref.at[:, i]


class Place:
    def __init__(self):
        gx, self.gy = lax.axis_index("gx"), lax.axis_index("gy")
        self.y, self.z = lax.div(gx, 4), lax.rem(gx, 4)
        self.x, self.c = lax.div(self.gy, 2), lax.rem(self.gy, 2)
        self.gx = gx

    def at(self, axis, k):
        return lax.rem((self.y if axis == "y" else self.z) + (k % 4), 4)

    def dev(self, axis, k):
        if axis == "y":
            return (self.at("y", k) * 4 + self.z, self.gy)
        return (self.y * 4 + self.at("z", k), self.gy)


class Stream:
    def __init__(self, here, first, s, p, far1, rel1, near1, mid, far2, rel2, near2, ss, rs):
        self.here, self.s, self.ss, self.rs = here, s, ss, rs
        self.ax = (first, "z" if first == "y" else "y")
        self.p, self.mid = p, mid
        self.far, self.rel, self.near = (far1, far2), (rel1, rel2), (near1, near2)

    def own(self, ph, k):
        at = self.here.at(self.ax[ph], k)
        return chunk(self.p, self.ax[0], at) if ph == 0 else self.mid.at[at]

    def copy(self, ph, i, direct=False):
        s = self.s
        src, dst, k = (
            (self.own(ph, 2), self.far[ph], 2 if direct else s),
            (self.own(ph, -s), self.near[ph], -s),
            (self.own(ph, s) if direct else self.far[ph], self.rel[ph], s),
        )[i]
        return pltpu.make_async_remote_copy(
            src, dst, self.ss.at[ph * 3 + i], self.rs.at[ph * 3 + i],
            device_id=self.here.dev(self.ax[ph], k), device_id_type=MESH,
        )

    def start(self, ph, direct=False):
        self.copy(ph, 0, direct).start()
        self.copy(ph, 1).start()
        if direct:
            self.copy(ph, 2, direct).start()

    def relay(self, ph):
        self.copy(ph, 0).wait_recv()
        ref = self.far[ph]
        ref[...] = (f32(ref[...]) + f32(self.own(ph, self.s)[...])).astype(ref.dtype)
        self.copy(ph, 2).start()

    def total(self, ph, direct=False):
        value = f32(self.own(ph, 0)[...])
        if direct:
            self.copy(ph, 0, direct).wait_recv()
            value += f32(self.far[ph][...])
        self.copy(ph, 1).wait_recv()
        self.copy(ph, 2, direct).wait_recv()
        return value + f32(self.rel[ph][...]) + f32(self.near[ph][...])

    def turn(self, direct=False):
        self.mid[...] = self.total(0).astype(self.mid.dtype)
        self.start(1, direct)

    def drain(self):
        for ph in (0, 1):
            for i in range(3):
                self.copy(ph, i).wait_send()


def kernel(
    stream_h, gain_h, wg_h, wu_h, wq_h, wkv_h, k_h, v_h, lengths,
    hidden, context,
    stream, gain, wg, wu, wq, wkv, kc, vc, load_sem, wsem,
    nsend, ybuf, zbuf, a8, xr, perm, xs,
    d_ss, d_rs, x_ss, x_rs, p_ss, p_rs,
    fp, ff1, fr1, fn1, fm, ff2, fr2, fn2, f_ss, f_rs,
    qp, qf1, qr1, qn1, qm, qf2, qr2, qn2,
    vp, vf1, vr1, vn1, vm, vf2, vr2, vn2, a_ss, a_rs,
    qs, qr, qa, kvs, g_ss, g_rs,
):
    h = Place()
    loads = [
        pltpu.make_async_copy(src, dst, load_sem.at[i])
        for i, (src, dst) in enumerate([(stream_h, stream), (gain_h, gain), (wq_h, wq), (wkv_h, wkv), (k_h, kc), (v_h, vc)])
    ]
    for c in loads[:4]:
        c.start()

    def wload(t):
        cols = pl.ds(pl.multiple_of(t * W, 128), W)
        return (
            pltpu.make_async_copy(wg_h.at[:, cols], wg.at[t], wsem.at[t, 0]),
            pltpu.make_async_copy(wu_h.at[:, cols], wu.at[t], wsem.at[t, 1]),
        )

    @pl.loop(0, T)
    def _(t):
        for c in wload(t):
            c.start()

    for c in loads[4:]:
        c.start()

    bar = pltpu.get_barrier_semaphore()
    for ax in "yz":
        for k in (1, 2, 3):
            pl.semaphore_signal(bar, inc=1, device_id=h.dev(ax, k), device_id_type=MESH)
    for k in range(1, 8):
        pl.semaphore_signal(bar, inc=1, device_id=(h.gx, lax.rem(h.gy + k, 8)), device_id_type=MESH)

    i = lax.broadcasted_iota(jnp.int32, (256, 256), 0)
    j = lax.broadcasted_iota(jnp.int32, (256, 256), 1)
    want = ((i >> 1) & 7) * 32 + ((i >> 4) & 3) * 8 + (i >> 6) * 2 + (i & 1)
    perm[...] = jnp.where(want == j, 1.0, 0.0).astype(BF16)
    vp[...] = jnp.zeros_like(vp)

    loads[0].wait()
    loads[1].wait()
    total = jnp.zeros((2, K), F32)
    for q in range(16):
        total += f32(stream[:, q * K:(q + 1) * K])
    mean = jnp.sum(total, axis=1, keepdims=True) * (1.0 / D)
    total = jnp.zeros((2, K), F32)
    for q in range(16):
        v = f32(stream[:, q * K:(q + 1) * K]) - mean
        total += v * v
    root = jnp.sqrt(jnp.sum(total, axis=1, keepdims=True) * (1.0 / D) + 1e-05)
    for q in range(16):
        v = (f32(stream[:, q * K:(q + 1) * K]) - mean) / root * gain[:, q * K:(q + 1) * K]
        nsend[q // 4, :, (q % 4) * K:(q % 4 + 1) * K] = v.astype(BF16)

    pl.semaphore_wait(bar, 13)

    first = [
        pltpu.make_async_remote_copy(
            nsend.at[h.at("y", k)], ybuf.at[h.y], d_ss.at[k], d_rs.at[k],
            device_id=h.dev("y", k), device_id_type=MESH)
        for k in (2, 1, 3)
    ]
    for c in first:
        c.start()
    ybuf[h.y] = nsend[h.y]
    for c in first:
        c.wait_recv()

    def zcols(zd):
        return pl.ds(pl.multiple_of(zd * K, 128), K)

    second = [
        pltpu.make_async_remote_copy(
            ybuf.at[:, :, zcols(h.at("z", k))], zbuf.at[h.z], d_ss.at[3 + k], d_rs.at[3 + k],
            device_id=h.dev("z", k), device_id_type=MESH)
        for k in (2, 1, 3)
    ]
    for c in second:
        c.start()

    def along(k):
        return lax.rem(h.gy + 2 * k, 8)

    def remote(src, dst, ss, rs, gy):
        return pltpu.make_async_remote_copy(
            src, dst, ss, rs, device_id=(h.gx, gy), device_id_type=MESH)

    def to_x(n, k):
        z = h.at("z", n)
        return remote(xr.at[h.gy, z], xr.at[h.gy, z], x_ss.at[n, k - 1], x_rs.at[n, k - 1], along(k))

    def to_partner(n, k):
        g, z = along(4 - k), h.at("z", n)
        return remote(xr.at[g, z], xr.at[g, z], p_ss.at[n, k], p_rs.at[n, k], h.x * 2 + 1 - h.c)

    for n in (0, 1, 3, 2):
        z = h.at("z", n)
        if n == 0:
            for y in range(4):
                a8[n, 2 * y:2 * y + 2, :] = f32(ybuf[y, :, zcols(h.z)])
        else:
            second[{2: 0, 1: 1, 3: 2}[4 - n]].wait_recv()
            for y in range(4):
                a8[n, 2 * y:2 * y + 2, :] = f32(zbuf[z, y])
        xr[h.gy, z] = a8[n].astype(BF16)
        for k in (2, 1, 3):
            to_x(n, k).start()
        to_partner(n, 0).start()
    for n in (0, 1, 3, 2):
        for k in (1, 3, 2):
            to_x(n, k).wait_recv()
            to_partner(n, k).start()
    for n in (0, 1, 3, 2):
        for k in range(4):
            to_partner(n, k).wait_recv()
    for n in range(3):
        cols = slice(n * 384, (n + 1) * 384)
        xs[:, cols] = jnp.dot(
            perm[...], xr[:, :, :, cols].reshape(256, 384), preferred_element_type=F32
        ).astype(BF16)
    for c in first + second:
        c.wait_send()
    for n in range(4):
        for k in (1, 2, 3):
            to_x(n, k).wait_send()
        for k in range(4):
            to_partner(n, k).wait_send()

    att = [
        Stream(h, first, s, qp.at[n], qf1.at[n], qr1.at[n], qn1.at[n], qm.at[n], qf2.at[n], qr2.at[n], qn2.at[n],
               a_ss.at[n], a_rs.at[n])
        for n, (first, s) in enumerate([("y", -1), ("z", 1), ("y", 1)])
    ]
    att.append(Stream(h, "z", -1, vp, vf1, vr1, vn1, vm, vf2, vr2, vn2, a_ss.at[3], a_rs.at[3]))

    def ffn(t, n, order):
        return Stream(h, order, -1 if n == 0 else 1, fp.at[t, n], ff1.at[t, n], fr1.at[t, n], fn1.at[t, n],
                      fm.at[t, n], ff2.at[t, n], fr2.at[t, n], fn2.at[t, n], f_ss.at[t, n], f_rs.at[t, n])

    def pair(i, do):
        for t, order in ((2 * i, "y"), (2 * i + 1, "z")):
            do(t, [ffn(t, n, order) for n in (0, 1)])

    loads[2].wait()
    loads[3].wait()
    query = jnp.dot(xs[...], wq[...], preferred_element_type=F32)
    for n in range(3):
        qp[n] = query[:, n * DH:(n + 1) * DH].reshape(4, 4, 16, DH)
    vp[:, :, :, 0:64] = lax.dot_general(
        xs[...], wkv[...], (((1,), (1,)), ((), ())), preferred_element_type=F32
    ).reshape(4, 4, 16, 64)
    for s in att:
        s.start(0)

    def computes(lo, hi):
        @pl.loop(lo, hi)
        def _(i):
            pair(i, lambda t, ss: [c.wait() for c in wload(t)])
            for t in (2 * i, 2 * i + 1):
                for n, w in ((0, wg), (1, wu)):
                    fp[t, n] = jnp.dot(xs[...], w[t], preferred_element_type=F32).astype(BF16).reshape(4, 4, 16, W)
            pair(i, lambda t, ss: [s.start(0) for s in ss])

    def each(lo, hi, do):
        @pl.loop(lo, hi)
        def _(i):
            pair(i, lambda t, ss: [do(s) for s in ss])

    computes(0, 2)
    for s in att:
        s.relay(0)
    computes(2, T // 2)
    for s in att:
        s.turn(True)
    each(0, T // 2, lambda s: s.relay(0))
    each(0, DIRECT, lambda s: s.turn())
    each(DIRECT, T // 2, lambda s: s.turn(True))

    for n, s in enumerate(att):
        val = s.total(1, True)
        for g in range(8):
            qs[g, :, n * DH:n * DH + val.shape[1]] = val[2 * g:2 * g + 2, :].astype(BF16)
    give = [
        pltpu.make_async_remote_copy(
            qs.at[lax.rem(h.gy + k, 8)], qr.at[h.gy], g_ss.at[k], g_rs.at[k],
            device_id=(h.gx, lax.rem(h.gy + k, 8)), device_id_type=MESH)
        for k in range(1, 8)
    ]
    for c in give:
        c.start()
    qr[h.gy] = qs[h.gy]

    each(0, DIRECT, lambda s: s.relay(1))

    for c in give:
        c.wait_recv()
    for g in range(8):
        for n in range(3):
            row = f32(qr[g, :, n * DH:(n + 1) * DH])
            for r in range(2):
                qa[r, g * 3 + n:g * 3 + n + 1, :] = row[r:r + 1, :]
        kvs[2 * g:2 * g + 2, :] = f32(qr[g, :, 768:896])
    moved = pltpu.roll(kvs[...], 64, axis=1)

    def whole(r, first):
        row = [(kvs[2 * g + r:2 * g + r + 1, :], moved[2 * g + r:2 * g + r + 1, :]) for g in range(first, first + 4)]
        return jnp.concatenate([row[0][0] + row[1][1], row[2][0] + row[3][1]], axis=1)

    loads[4].wait()
    loads[5].wait()
    scale = DH ** (-0.5)
    for r in range(2):
        query = qa[r]
        scores = lax.dot_general(
            query.astype(BF16), kc[r], (((1,), (1,)), ((), ())), preferred_element_type=F32) * scale
        score_new = jnp.sum(query * whole(r, 0), axis=1, keepdims=True) * scale
        mask = lax.broadcasted_iota(jnp.int32, (HEADS, CACHE), 1) < lengths[r]
        top = jnp.maximum(jnp.max(jnp.where(mask, scores, -1e30), axis=1, keepdims=True), score_new)
        exponent = jnp.where(mask, jnp.exp(scores - top), 0.0)
        exponent_new = jnp.exp(score_new - top)
        total = jnp.sum(exponent, axis=1, keepdims=True) + exponent_new
        weights = (exponent / total).astype(BF16)
        weights_new = f32((exponent_new / total).astype(BF16))
        out = jnp.dot(weights, vc[r], preferred_element_type=F32) + weights_new * whole(r, 4)
        context[r] = out.astype(BF16)

    def finish(direct, t, ss):
        gate, up = ss[0].total(1, direct), ss[1].total(1, direct)
        cols = pl.ds(pl.multiple_of(t * W, 128), W)
        hidden[:, cols] = (gate / (1.0 + jnp.exp(-gate)) * up).astype(BF16)

    @pl.loop(0, DIRECT)
    def _(i):
        pair(i, functools.partial(finish, False))

    @pl.loop(DIRECT, T // 2)
    def _(i):
        pair(i, functools.partial(finish, True))

    for c in give:
        c.wait_send()
    for s in att:
        s.drain()

    each(0, T // 2, lambda s: s.drain())


def fused(stream, gain, w_gate, w_up, w_query, w_keyval, k_cache, v_cache, lengths):
    vm, dma = pltpu.VMEM, pltpu.SemaphoreType.DMA

    def rs(lead, wide, kind):
        return [
            vm(lead + (4, 4, 16, wide), kind),
            *[vm(lead + (4, 16, wide), kind)] * 3,
            vm(lead + (4, 16, wide), kind),
            *[vm(lead + (16, wide), kind)] * 3,
        ]

    return pl.pallas_call(
        kernel,
        out_shape=(
            jax.ShapeDtypeStruct((16, FF), BF16),
            jax.ShapeDtypeStruct((2, HEADS, DH), BF16),
        ),
        in_specs=[pl.BlockSpec(memory_space=pl.ANY)] * 8 + [pl.BlockSpec(memory_space=pltpu.SMEM)],
        out_specs=[pl.BlockSpec(memory_space=pltpu.VMEM)] * 2,
        scratch_shapes=[
            vm((2, D), BF16), vm((1, D), F32), vm((T, K, W), BF16), vm((T, K, W), BF16),
            vm((K, 768), BF16), vm((64, K), BF16), vm((2, CACHE, DH), BF16), vm((2, CACHE, DH), BF16),
            dma((6,)), dma((T, 2)),
            vm((4, 2, 4 * K), BF16), vm((4, 2, 4 * K), BF16), vm((4, 4, 2, K), BF16), vm((4, 8, K), F32),
            vm((8, 4, 8, K), BF16), vm((256, 256), BF16), vm((256, K), BF16),
            dma((7,)), dma((7,)), dma((4, 3)), dma((4, 3)), dma((4, 4)), dma((4, 4)),
            *rs((T, 2), W, BF16), dma((T, 2, 6)), dma((T, 2, 6)),
            *rs((3,), DH, F32),
            *rs((), 128, F32), dma((4, 6)), dma((4, 6)),
            vm((8, 2, 896), BF16), vm((8, 2, 896), BF16), vm((2, HEADS, DH), F32), vm((16, 128), F32),
            dma((8,)), dma((8,)),
        ],
        compiler_params=pltpu.CompilerParams(
            collective_id=0, has_side_effects=True, vmem_limit_bytes=62 * 2**20
        ),
    )(stream, gain, w_gate, w_up, w_query, w_keyval, k_cache, v_cache, lengths)


def body(stream, norm_gain, w_gate, w_up, w_query, w_keyval, k_cache, v_cache, lengths):
    hidden, context = fused(
        stream, norm_gain.reshape(1, D), w_gate, w_up, w_query, w_keyval.T, k_cache, v_cache, lengths
    )
    return (hidden, context.reshape(2, HEADS * DH))


def solution(mesh):
    return jax.shard_map(
        body,
        mesh=mesh,
        in_specs=(
            P(("gx", "gy"), None),
            P(),
            P("gx", "gy"),
            P("gx", "gy"),
            P("gx", "gy"),
            P("gx", "gy"),
            P(("gx", "gy"), None, None),
            P(("gx", "gy"), None, None),
            P(("gx", "gy")),
        ),
        out_specs=(P("gx", "gy"), P(("gx", "gy"), None)),
        check_vma=False,
    )
```

time: 68.8 us -> 62.9 us (0.914); the launches traced: 67.5 us -> 62.7 us
  local copies, waits for them, and re-layouts: 5.63 us -> 2.94 us
  Pallas kernels: 60.2 us -> 59.2 us
  matrix products: 0.7 us -> 0 us
    slice x4 -> x0, local copies, waits for them, and re-layouts: 1.45 us -> none  [the longest x2 0.76 us: body(): query = pieces[:, :, :768].reshape(rows, HEADS, DH)]
    unnamed x9 -> x2, local copies, waits for them, and re-layouts: 4.08 us -> 2.94 us
    pallas_call x1, Pallas kernels: 60.2 us -> 59.2 us  [fused(): pl.pallas_call(kernel, out_shape=(jax.ShapeDtypeStruct((16, FF), BF16), j...]
    dot_general x3 -> x0, matrix products: 0.7 us -> none  [the longest x1 0.33 us: body(): jnp.einsum('bhd,bld->bhl', query, k_cache, preferred_element_type=F32)]
where the time goes in v2:
time: 62.9 us; the launch traced here: 62.7 us
  Pallas kernels  59.2 us (94%)
  local copies, waits for them, and re-layouts  2.94 us (5%)
  between operations  0.64 us (1%)
    pallas_call x1, Pallas kernels, fused(): pl.pallas_call(kernel, out_shape=(jax.ShapeDtypeStruct((16, FF), BF16), j...  59.2 us
    unnamed x2, local copies, waits for them, and re-layouts  2.94 us

profile of v2, /device:TPU:1, one launch (start us, length us, event | category | flops | bytes accessed | tf_op | source)
XLA Modules:
  0.0 62.7 jit_solution(6599225070370915147)
XLA Ops:
  0.6 59.2 %shard_map.104 = (bf16[16,4608]{1,0:T(8,128)(2,1)}, bf16[2,24,256]{2,1,0:T(8,128)(2,1)}) custom-call(bf16[2,18432]{1,0:T(2,128)(2,1)} %stream_h.1, f32[1,18432]{1,0:T(1,128)} %bitcast.5, bf16[1152,4608]{1,0:T(8,128)(2,1)} %wg_h.1, bf16[1152,4608]{1,0:T(8,128)(2,1)} %wu_h.1, bf16[1152,768]{1,0:T(8,128)(2,1)} %wq_h.1, bf16[64,1152]{1,0:T(8,128)(2,1)} %bitcast.4, ...), custom_call_target="tpu_custom_call" | custom-call | tf_op jit(solution)/shard_map/pallas_call | solution.py:368
  59.8 1.4 %copy.11 = bf16[1,2,24,256]{3,1,2,0:T(2,128)(2,1)} copy(bf16[1,2,24,256]{3,2,1,0:T(8,128)(2,1)} %bitcast.7) | data formatting | bytes 49152
  61.2 1.6 %copy.13 = bf16[16,4608]{1,0:T(8,128)(2,1)} copy(bf16[16,4608]{1,0:T(8,128)(2,1)} %get-tuple-element.8) | data formatting | bytes 294912

commit v3 on v2

--- a/solution.py
+++ b/solution.py
@@ -100,9 +100,9 @@
 
 
 def kernel(
-    stream_h, gain_h, wg_h, wu_h, wq_h, wkv_h, k_h, v_h, lengths,
+    stream_h, gain_h, wg_h, wu_h, wq_h, wkv_h, k_h, v_h, lengths_h,
     hidden, context,
-    stream, gain, wg, wu, wq, wkv, kc, vc, load_sem, wsem,
+    stream, gain, wg, wu, wq, wkv, kc, vc, lengths, load_sem, wsem,
     nsend, ybuf, zbuf, a8, xr, perm, xs,
     d_ss, d_rs, x_ss, x_rs, p_ss, p_rs,
     fp, ff1, fr1, fn1, fm, ff2, fr2, fn2, f_ss, f_rs,
@@ -111,9 +111,16 @@
     qs, qr, qa, kvs, g_ss, g_rs,
 ):
     h = Place()
+    bar = pltpu.get_barrier_semaphore()
+    for ax in "yz":
+        for k in (1, 2, 3):
+            pl.semaphore_signal(bar, inc=1, device_id=h.dev(ax, k), device_id_type=MESH)
+    for k in range(1, 8):
+        pl.semaphore_signal(bar, inc=1, device_id=(h.gx, lax.rem(h.gy + k, 8)), device_id_type=MESH)
+
     loads = [
         pltpu.make_async_copy(src, dst, load_sem.at[i])
-        for i, (src, dst) in enumerate([(stream_h, stream), (gain_h, gain), (wq_h, wq), (wkv_h, wkv), (k_h, kc), (v_h, vc)])
+        for i, (src, dst) in enumerate([(stream_h, stream), (gain_h, gain), (wq_h, wq), (wkv_h, wkv), (k_h, kc), (v_h, vc), (lengths_h, lengths)])
     ]
     for c in loads[:4]:
         c.start()
@@ -132,19 +139,6 @@
 
     for c in loads[4:]:
         c.start()
-
-    bar = pltpu.get_barrier_semaphore()
-    for ax in "yz":
-        for k in (1, 2, 3):
-            pl.semaphore_signal(bar, inc=1, device_id=h.dev(ax, k), device_id_type=MESH)
-    for k in range(1, 8):
-        pl.semaphore_signal(bar, inc=1, device_id=(h.gx, lax.rem(h.gy + k, 8)), device_id_type=MESH)
-
-    i = lax.broadcasted_iota(jnp.int32, (256, 256), 0)
-    j = lax.broadcasted_iota(jnp.int32, (256, 256), 1)
-    want = ((i >> 1) & 7) * 32 + ((i >> 4) & 3) * 8 + (i >> 6) * 2 + (i & 1)
-    perm[...] = jnp.where(want == j, 1.0, 0.0).astype(BF16)
-    vp[...] = jnp.zeros_like(vp)
 
     loads[0].wait()
     loads[1].wait()
@@ -161,6 +155,12 @@
         v = (f32(stream[:, q * K:(q + 1) * K]) - mean) / root * gain[:, q * K:(q + 1) * K]
         nsend[q // 4, :, (q % 4) * K:(q % 4 + 1) * K] = v.astype(BF16)
 
+    i = lax.broadcasted_iota(jnp.int32, (256, 256), 0)
+    j = lax.broadcasted_iota(jnp.int32, (256, 256), 1)
+    want = ((i >> 1) & 7) * 32 + ((i >> 4) & 3) * 8 + (i >> 6) * 2 + (i & 1)
+    perm[...] = jnp.where(want == j, 1.0, 0.0).astype(BF16)
+    vp[...] = jnp.zeros_like(vp)
+
     pl.semaphore_wait(bar, 13)
 
     first = [
@@ -198,7 +198,13 @@
         z = h.at("z", n)
         return remote(xr.at[h.gy, z], xr.at[h.gy, z], x_ss.at[n, k - 1], x_rs.at[n, k - 1], along(k))
 
+    def to_other(k):
+        z = h.at("z", 2)
+        return remote(xr.at[h.gy, z], xr.at[h.gy, z], p_ss.at[2, k], p_rs.at[2, k], along(k) + 1 - 2 * h.c)
+
     def to_partner(n, k):
+        if n == 2 and k:
+            return to_other(k)
         g, z = along(4 - k), h.at("z", n)
         return remote(xr.at[g, z], xr.at[g, z], p_ss.at[n, k], p_rs.at[n, k], h.x * 2 + 1 - h.c)
 
@@ -214,11 +220,14 @@
         xr[h.gy, z] = a8[n].astype(BF16)
         for k in (2, 1, 3):
             to_x(n, k).start()
+            if n == 2:
+                to_partner(n, k).start()
         to_partner(n, 0).start()
     for n in (0, 1, 3, 2):
         for k in (1, 3, 2):
             to_x(n, k).wait_recv()
-            to_partner(n, k).start()
+            if n != 2:
+                to_partner(n, k).start()
     for n in (0, 1, 3, 2):
         for k in range(4):
             to_partner(n, k).wait_recv()
@@ -227,14 +236,6 @@
         xs[:, cols] = jnp.dot(
             perm[...], xr[:, :, :, cols].reshape(256, 384), preferred_element_type=F32
         ).astype(BF16)
-    for c in first + second:
-        c.wait_send()
-    for n in range(4):
-        for k in (1, 2, 3):
-            to_x(n, k).wait_send()
-        for k in range(4):
-            to_partner(n, k).wait_send()
-
     att = [
         Stream(h, first, s, qp.at[n], qf1.at[n], qr1.at[n], qn1.at[n], qm.at[n], qf2.at[n], qr2.at[n], qn2.at[n],
                a_ss.at[n], a_rs.at[n])
@@ -275,13 +276,14 @@
         def _(i):
             pair(i, lambda t, ss: [do(s) for s in ss])
 
-    computes(0, 2)
+    computes(0, 3)
     for s in att:
         s.relay(0)
-    computes(2, T // 2)
+    computes(3, T // 2)
+    each(0, 3, lambda s: s.relay(0))
     for s in att:
         s.turn(True)
-    each(0, T // 2, lambda s: s.relay(0))
+    each(3, T // 2, lambda s: s.relay(0))
     each(0, DIRECT, lambda s: s.turn())
     each(DIRECT, T // 2, lambda s: s.turn(True))
 
@@ -298,7 +300,6 @@
     for c in give:
         c.start()
     qr[h.gy] = qs[h.gy]
-
     each(0, DIRECT, lambda s: s.relay(1))
 
     for c in give:
@@ -315,8 +316,8 @@
         row = [(kvs[2 * g + r:2 * g + r + 1, :], moved[2 * g + r:2 * g + r + 1, :]) for g in range(first, first + 4)]
         return jnp.concatenate([row[0][0] + row[1][1], row[2][0] + row[3][1]], axis=1)
 
-    loads[4].wait()
-    loads[5].wait()
+    for c in loads[4:]:
+        c.wait()
     scale = DH ** (-0.5)
     for r in range(2):
         query = qa[r]
@@ -331,7 +332,8 @@
         weights = (exponent / total).astype(BF16)
         weights_new = f32((exponent_new / total).astype(BF16))
         out = jnp.dot(weights, vc[r], preferred_element_type=F32) + weights_new * whole(r, 4)
-        context[r] = out.astype(BF16)
+        for n in range(HEADS):
+            context[r:r + 1, n * DH:(n + 1) * DH] = out[n:n + 1, :].astype(BF16)
 
     def finish(direct, t, ss):
         gate, up = ss[0].total(1, direct), ss[1].total(1, direct)
@@ -346,6 +348,13 @@
     def _(i):
         pair(i, functools.partial(finish, True))
 
+    for c in first + second:
+        c.wait_send()
+    for n in range(4):
+        for k in (1, 2, 3):
+            to_x(n, k).wait_send()
+        for k in range(4):
+            to_partner(n, k).wait_send()
     for c in give:
         c.wait_send()
     for s in att:
@@ -368,15 +377,15 @@
     return pl.pallas_call(
         kernel,
         out_shape=(
-            jax.ShapeDtypeStruct((16, FF), BF16),
-            jax.ShapeDtypeStruct((2, HEADS, DH), BF16),
+            vm((16, FF), BF16),
+            vm((2, HEADS * DH), BF16),
         ),
-        in_specs=[pl.BlockSpec(memory_space=pl.ANY)] * 8 + [pl.BlockSpec(memory_space=pltpu.SMEM)],
+        in_specs=[pl.BlockSpec(memory_space=pl.ANY)] * 9,
         out_specs=[pl.BlockSpec(memory_space=pltpu.VMEM)] * 2,
         scratch_shapes=[
             vm((2, D), BF16), vm((1, D), F32), vm((T, K, W), BF16), vm((T, K, W), BF16),
             vm((K, 768), BF16), vm((64, K), BF16), vm((2, CACHE, DH), BF16), vm((2, CACHE, DH), BF16),
-            dma((6,)), dma((T, 2)),
+            pltpu.SMEM((2,), jnp.int32), dma((7,)), dma((T, 2)),
             vm((4, 2, 4 * K), BF16), vm((4, 2, 4 * K), BF16), vm((4, 4, 2, K), BF16), vm((4, 8, K), F32),
             vm((8, 4, 8, K), BF16), vm((256, 256), BF16), vm((256, K), BF16),
             dma((7,)), dma((7,)), dma((4, 3)), dma((4, 3)), dma((4, 4)), dma((4, 4)),
@@ -396,7 +405,7 @@
     hidden, context = fused(
         stream, norm_gain.reshape(1, D), w_gate, w_up, w_query, w_keyval.T, k_cache, v_cache, lengths
     )
-    return (hidden, context.reshape(2, HEADS * DH))
+    return (hidden, context)
 
 
 def solution(mesh):

time: 62.9 us -> 59.3 us (0.943)
  Pallas kernels: 59.2 us -> 57.3 us
  local copies, waits for them, and re-layouts: 2.94 us -> 1.27 us
    pallas_call x1, Pallas kernels: 59.2 us -> 57.3 us  [fused(): pl.pallas_call(kernel, out_shape=(vm((16, FF), BF16), vm((2, HEADS * DH),...]
    unnamed x2, local copies, waits for them, and re-layouts: 2.94 us -> 1.27 us
where the time goes in v3:
time: 59.3 us; the launch traced here: 59.2 us
  Pallas kernels  57.3 us (97%)
  local copies, waits for them, and re-layouts  1.27 us (2%)
  between operations  0.64 us (1%)
    pallas_call x1, Pallas kernels, fused(): pl.pallas_call(kernel, out_shape=(vm((16, FF), BF16), vm((2, HEADS * DH),...  57.3 us
    unnamed x2, local copies, waits for them, and re-layouts  1.27 us

profile of v3, /device:TPU:1, one launch (start us, length us, event | category | flops | bytes accessed | tf_op | source)
XLA Modules:
  0.0 59.2 jit_solution(16907538757805978001)
XLA Ops:
  0.6 57.3 %shard_map.104 = (bf16[16,4608]{1,0:T(8,128)(2,1)S(1)}, bf16[2,6144]{1,0:T(2,128)(2,1)S(1)}) custom-call(bf16[2,18432]{1,0:T(2,128)(2,1)} %stream_h.1, f32[1,18432]{1,0:T(1,128)} %bitcast.3, bf16[1152,4608]{1,0:T(8,128)(2,1)} %wg_h.1, bf16[1152,4608]{1,0:T(8,128)(2,1)} %wu_h.1, bf16[1152,768]{1,0:T(8,128)(2,1)} %wq_h.1, bf16[64,1152]{1,0:T(8,128)(2,1)} %bitcast.2, ...), custom_call_target="tpu_custom_call" | custom-call | tf_op jit(solution)/shard_map/pallas_call | solution.py:377
  57.9 0.7 %copy.13 = bf16[16,4608]{1,0:T(8,128)(2,1)} copy(bf16[16,4608]{1,0:T(8,128)(2,1)S(1)} %get-tuple-element.2) | data formatting | bytes 294912
  58.6 0.6 %copy.14 = bf16[2,6144]{1,0:T(2,128)(2,1)} copy(bf16[2,6144]{1,0:T(2,128)(2,1)S(1)} %get-tuple-element.3) | data formatting | bytes 49152

commit v4 on v3

v4 whole, which is shorter than its diff:
```python
import functools

import jax
import jax.numpy as jnp
from jax import lax
from jax.experimental import pallas as pl
from jax.experimental.pallas import tpu as pltpu
from jax.sharding import PartitionSpec as P

HEADS = 24
DH = 256
D = 18432
K = 1152
FF = 4608
T = 12
DIRECT = 4
CACHE = 512
W = FF // T
MESH = pl.DeviceIdType.MESH
F32 = jnp.float32
BF16 = jnp.bfloat16


def f32(v):
    return v.astype(F32)


class Place:
    def __init__(self):
        gx, self.gy = lax.axis_index("gx"), lax.axis_index("gy")
        self.y, self.z = lax.div(gx, 4), lax.rem(gx, 4)
        self.x, self.c = lax.div(self.gy, 2), lax.rem(self.gy, 2)
        self.gx = gx

    def at(self, axis, k):
        return lax.rem((self.y if axis == "y" else self.z) + (k % 4), 4)

    def dev(self, axis, k):
        if axis == "y":
            return (self.at("y", k) * 4 + self.z, self.gy)
        return (self.y * 4 + self.at("z", k), self.gy)


class Stream:
    def __init__(self, here, first, s, p, mid, far, rel, near, tmp, ss, rs):
        self.here, self.s, self.ss, self.rs = here, s, ss, rs
        second = "z" if first == "y" else "y"
        self.ax = (first, first, second)
        self.p, self.mid, self.tmp = p, mid, tmp
        self.far, self.rel, self.near = far, rel, near

    def own(self, ph, k):
        return (*self.p, self.mid)[ph].at[self.here.at(self.ax[ph], k)]

    def copy(self, ph, i, direct=False):
        s = self.s
        src, dst, k = (
            (self.own(ph, 2), self.far[ph], 2 if direct else s),
            (self.own(ph, -s), self.near[ph], -s),
            (self.own(ph, s) if direct else self.far[ph], self.rel[ph], s),
        )[i]
        return pltpu.make_async_remote_copy(
            src, dst, self.ss.at[ph * 3 + i], self.rs.at[ph * 2 + (i > 0)],
            device_id=self.here.dev(self.ax[ph], k), device_id_type=MESH,
        )

    def start(self, ph, direct=False):
        self.copy(ph, 0, direct).start()
        self.copy(ph, 1).start()
        if direct:
            self.copy(ph, 2, direct).start()

    def relay(self, ph):
        ref = self.far[ph]
        ref[...] = (f32(ref[...]) + f32(self.own(ph, self.s)[...])).astype(ref.dtype)
        self.copy(ph, 2).start()

    def total(self, ph, direct=False):
        value = f32(self.own(ph, 0)[...])
        if direct:
            value += f32(self.far[ph][...])
        return value + f32(self.rel[ph][...]) + f32(self.near[ph][...])

    def turn(self, direct=False):
        small, large = self.total(0), self.total(1)
        cols = slice(0, small.shape[1])
        for i in range(4):
            self.tmp[i, 0:4, cols] = small[4 * i:4 * i + 4]
            self.tmp[i, 4:16, cols] = large[12 * i:12 * i + 12]
        self.mid[...] = self.tmp[:, :, cols].astype(self.mid.dtype)
        self.start(2, direct)


def kernel(
    stream_h, gain_h, wg_h, wu_h, wq_h, wkv_h, k_h, v_h, lengths_h,
    hidden, context,
    stream, gain, wgu, wq, wkv, kc, vc, lengths, load_sem, wsem,
    nsend, ybuf, zbuf, a8, xr, perm0, perm1, xs0, xs1, tmp,
    d_ss, d_rs,
    *rest,
):
    fb, qb, vb = rest[0:9], rest[9:18], rest[18:27]
    f_ss, f_rs, q_ss, q_rs, v_ss, v_rs, qs, qr, qa, kvs, g_ss, g_rs = rest[27:]
    perm, xs = (perm0, perm1), (xs0, xs1)
    h = Place()
    bar = pltpu.get_barrier_semaphore()
    for ax in "yz":
        for k in (1, 2, 3):
            pl.semaphore_signal(bar, inc=1, device_id=h.dev(ax, k), device_id_type=MESH)
    for k in range(1, 8):
        pl.semaphore_signal(bar, inc=1, device_id=(h.gx, lax.rem(h.gy + k, 8)), device_id_type=MESH)

    loads = [
        pltpu.make_async_copy(src, dst, load_sem.at[i])
        for i, (src, dst) in enumerate([(stream_h, stream), (gain_h, gain), (wq_h, wq), (wkv_h, wkv), (k_h, kc), (v_h, vc), (lengths_h, lengths)])
    ]
    for c in loads[:4]:
        c.start()

    def wload(t):
        cols = pl.ds(pl.multiple_of(t * W, 128), W)
        return (
            pltpu.make_async_copy(wg_h.at[:, cols], wgu.at[t, 0], wsem.at[t // 2]),
            pltpu.make_async_copy(wu_h.at[:, cols], wgu.at[t, 1], wsem.at[t // 2]),
        )

    @pl.loop(0, T)
    def _(t):
        for c in wload(t):
            c.start()

    for c in loads[4:]:
        c.start()

    loads[0].wait()
    loads[1].wait()
    total = jnp.zeros((2, K), F32)
    for q in range(16):
        total += f32(stream[:, q * K:(q + 1) * K])
    mean = jnp.sum(total, axis=1, keepdims=True) * (1.0 / D)
    total = jnp.zeros((2, K), F32)
    for q in range(16):
        v = f32(stream[:, q * K:(q + 1) * K]) - mean
        total += v * v
    root = jnp.sqrt(jnp.sum(total, axis=1, keepdims=True) * (1.0 / D) + 1e-05)
    for q in range(16):
        v = (f32(stream[:, q * K:(q + 1) * K]) - mean) / root * gain[:, q * K:(q + 1) * K]
        nsend[q // 4, :, (q % 4) * K:(q % 4 + 1) * K] = v.astype(BF16)

    for part, m in ((0, 4), (1, 12)):
        i = lax.broadcasted_iota(jnp.int32, (16 * m, 16 * m), 0)
        j = lax.broadcasted_iota(jnp.int32, (16 * m, 16 * m), 1)
        y, z = (j >> 1) & 3, (j >> 3) & 3
        rest_of = (j >> 6) * 4 + ((j >> 5) & 1) * 2 + (j & 1)
        for order, (u, v) in enumerate(((y, z), (z, y))):
            perm[part][order] = jnp.where(i == u * (4 * m) + v * m + rest_of, 1.0, 0.0).astype(BF16)
    vb[0][...] = jnp.zeros_like(vb[0])
    vb[1][...] = jnp.zeros_like(vb[1])

    pl.semaphore_wait(bar, 13)

    def take(ref, sem):
        pltpu.make_async_remote_copy(
            ref, ref, sem, sem, device_id=h.dev("y", 1), device_id_type=MESH).wait_recv()

    def sent(ref, sem):
        pltpu.make_async_remote_copy(
            ref, ref, sem, sem, device_id=h.dev("y", 1), device_id_type=MESH).wait_send()

    first = [
        pltpu.make_async_remote_copy(
            nsend.at[h.at("y", k)], ybuf.at[h.y], d_ss.at[0], d_rs.at[0],
            device_id=h.dev("y", k), device_id_type=MESH)
        for k in (2, 1, 3)
    ]
    for c in first:
        c.start()
    ybuf[h.y] = nsend[h.y]
    take(ybuf.at[0:3], d_rs.at[0])

    def zcols(zd):
        return pl.ds(pl.multiple_of(zd * K, 128), K)

    second = [
        pltpu.make_async_remote_copy(
            ybuf.at[:, :, zcols(h.at("z", k))], zbuf.at[h.z], d_ss.at[1], d_rs.at[k],
            device_id=h.dev("z", k), device_id_type=MESH)
        for k in (2, 1, 3)
    ]
    for c in second:
        c.start()

    def along(k, flip):
        return lax.rem(h.x + k, 4) * 2 + lax.rem(h.c + flip, 2)

    def to_x(n, k, flip):
        z, slot = h.at("z", n), (4 - k) % 4
        return pltpu.make_async_remote_copy(
            xr.at[h.c, z], xr.at[slot * 2 + h.c, z], d_ss.at[2], d_rs.at[4 if k == 0 else 5],
            device_id=(h.gx, along(k, flip)), device_id_type=MESH)

    for n in (0, 1, 3, 2):
        z = h.at("z", n)
        if n == 0:
            for y in range(4):
                a8[n, 2 * y:2 * y + 2, :] = f32(ybuf[y, :, zcols(h.z)])
        else:
            second[{2: 0, 1: 1, 3: 2}[4 - n]].wait_recv()
            for y in range(4):
                a8[n, 2 * y:2 * y + 2, :] = f32(zbuf[z, y])
        xr[h.c, z] = a8[n].astype(BF16)
        for k, flip in ((0, 1), (3, 0), (3, 1), (2, 0), (2, 1), (1, 0), (1, 1)):
            to_x(n, k, flip).start()

    def rows(part):
        take(xr.at[0:(1, 6)[part]], d_rs.at[4 + part])
        for n in range(3):
            cols = slice(n * 384, (n + 1) * 384)
            got = xr[0:2, :, :, cols].reshape(64, 384) if part == 0 else xr[2:8, :, :, cols].reshape(192, 384)
            for order in (0, 1):
                xs[part][order, :, cols] = jnp.dot(
                    perm[part][order], got, preferred_element_type=F32).astype(BF16)

    def stream_of(b, lead, n, first, s, ss, rs):
        at = lead + (n,)
        return Stream(
            h, first, s, [b[0].at[at], b[1].at[at]], b[2].at[at], [r.at[at] for r in b[3:6]],
            [r.at[lead + (0, n)] for r in b[6:9]], [r.at[lead + (1, n)] for r in b[6:9]], tmp, ss, rs)

    att = [
        stream_of(qb, (), n, first, s, q_ss, q_rs)
        for n, (first, s) in enumerate([("y", -1), ("y", 1), ("z", 1)])
    ]
    att.append(stream_of(vb, (), 0, "z", -1, v_ss, v_rs))

    def att_take(ph, role):
        for b, sem in ((qb, q_rs), (vb, v_rs)):
            take(b[3 + 3 * role + ph], sem.at[ph * 2 + role])

    def pair_take(i, ph, role):
        take(fb[3 + 3 * role + ph].at[pl.ds(2 * i, 2)], f_rs.at[i, ph * 2 + role])

    def pair(i, do):
        for t, order in ((2 * i, "y"), (2 * i + 1, "z")):
            do(t, [stream_of(fb, (t,), n, order, -1 if n == 0 else 1, f_ss, f_rs.at[i]) for n in (0, 1)])

    def query(part):
        m = (16, 48)[part]
        val = jnp.dot(xs[part][0], wq[:, :2 * DH], preferred_element_type=F32)
        for n in range(2):
            qb[part][n] = val[:, n * DH:(n + 1) * DH].reshape(4, m, DH)
        qb[part][2] = jnp.dot(xs[part][1], wq[:, 2 * DH:], preferred_element_type=F32).reshape(4, m, DH)
        vb[part][0, :, :, 0:64] = lax.dot_general(
            xs[part][1], wkv[...], (((1,), (1,)), ((), ())), preferred_element_type=F32
        ).reshape(4, m, 64)
        for s in att:
            s.start(part)

    def computes(part, lo, hi):
        @pl.loop(lo, hi)
        def _(i):
            if part == 0:
                both = wgu.at[pl.ds(2 * i, 2)]
                pltpu.make_async_copy(both, both, wsem.at[i]).wait()
            for order in (0, 1):
                t = 2 * i + order
                for n in (0, 1):
                    val = jnp.dot(xs[part][order], wgu[t, n], preferred_element_type=F32)
                    fb[part][t, n] = val.astype(BF16).reshape(4, (16, 48)[part], W)
            pair(i, lambda t, ss: [s.start(part) for s in ss])

    def relays(ph, lo, hi):
        @pl.loop(lo, hi)
        def _(i):
            pair_take(i, ph, 0)
            pair(i, lambda t, ss: [s.relay(ph) for s in ss])

    def turns(lo, hi, direct):
        @pl.loop(lo, hi)
        def _(i):
            for ph in (0, 1):
                pair_take(i, ph, 1)
            pair(i, lambda t, ss: [s.turn(direct) for s in ss])

    def att_relay(ph):
        att_take(ph, 0)
        for s in att:
            s.relay(ph)

    rows(0)
    loads[2].wait()
    loads[3].wait()
    query(0)
    computes(0, 0, 4)
    att_relay(0)
    relays(0, 0, 2)
    computes(0, 4, T // 2)
    rows(1)
    query(1)
    computes(1, 0, 2)
    relays(0, 2, T // 2)
    computes(1, 2, 4)
    att_relay(1)
    computes(1, 4, T // 2)
    relays(1, 0, 3)
    for ph in (0, 1):
        att_take(ph, 1)
    for s in att:
        s.turn(True)
    relays(1, 3, T // 2)
    turns(0, DIRECT, False)
    turns(DIRECT, T // 2, True)

    att_take(2, 0)
    att_take(2, 1)
    for n, s in enumerate(att):
        val = s.total(2, True)
        for g in range(8):
            qs[g, :, n * DH:n * DH + val.shape[1]] = val[2 * g:2 * g + 2, :].astype(BF16)
    give = [
        pltpu.make_async_remote_copy(
            qs.at[2 * k + lax.rem(h.c + flip, 2)], qr.at[h.gy], g_ss.at[0], g_rs.at[0],
            device_id=(h.gx, along(k, flip)), device_id_type=MESH)
        for k in range(4) for flip in (0, 1) if k or flip
    ]
    for c in give:
        c.start()
    qr[h.gy] = qs[h.c]
    relays(2, 0, DIRECT)

    take(qr.at[0:7], g_rs.at[0])
    for g in range(8):
        for n in range(3):
            row = f32(qr[g, :, n * DH:(n + 1) * DH])
            for r in range(2):
                qa[r, g * 3 + n:g * 3 + n + 1, :] = row[r:r + 1, :]
        kvs[2 * g:2 * g + 2, :] = f32(qr[g, :, 768:896])
    moved = pltpu.roll(kvs[...], 64, axis=1)

    def whole(r, first):
        row = [(kvs[2 * g + r:2 * g + r + 1, :], moved[2 * g + r:2 * g + r + 1, :]) for g in range(first, first + 4)]
        return jnp.concatenate([row[0][0] + row[1][1], row[2][0] + row[3][1]], axis=1)

    for c in loads[4:]:
        c.wait()
    scale = DH ** (-0.5)
    for r in range(2):
        query = qa[r]
        scores = lax.dot_general(
            query.astype(BF16), kc[r], (((1,), (1,)), ((), ())), preferred_element_type=F32) * scale
        score_new = jnp.sum(query * whole(r, 0), axis=1, keepdims=True) * scale
        mask = lax.broadcasted_iota(jnp.int32, (HEADS, CACHE), 1) < lengths[r]
        top = jnp.maximum(jnp.max(jnp.where(mask, scores, -1e30), axis=1, keepdims=True), score_new)
        exponent = jnp.where(mask, jnp.exp(scores - top), 0.0)
        exponent_new = jnp.exp(score_new - top)
        total = jnp.sum(exponent, axis=1, keepdims=True) + exponent_new
        weights = (exponent / total).astype(BF16)
        weights_new = f32((exponent_new / total).astype(BF16))
        out = jnp.dot(weights, vc[r], preferred_element_type=F32) + weights_new * whole(r, 4)
        for n in range(HEADS):
            context[r:r + 1, n * DH:(n + 1) * DH] = out[n:n + 1, :].astype(BF16)

    def finish(direct, t, ss):
        gate, up = (s.total(2, direct) for s in ss)
        cols = pl.ds(pl.multiple_of(t * W, 128), W)
        val = gate / (1.0 + jnp.exp(-gate)) * up
        val = jnp.where(h.x % 2 == 1, jnp.roll(val, 4, axis=0), val)
        val = jnp.where(h.x >= 2, jnp.roll(val, 8, axis=0), val)
        hidden[:, cols] = val.astype(BF16)

    @pl.loop(0, DIRECT)
    def _(i):
        pair_take(i, 2, 1)
        pair(i, functools.partial(finish, False))

    @pl.loop(DIRECT, T // 2)
    def _(i):
        pair_take(i, 2, 0)
        pair_take(i, 2, 1)
        pair(i, functools.partial(finish, True))

    sent(ybuf.at[0:3], d_ss.at[0])
    sent(zbuf.at[0:3], d_ss.at[1])
    sent(xr.at[0:7], d_ss.at[2])
    sent(qr.at[0:7], g_ss.at[0])
    for b, ss in ((fb, f_ss), (qb, q_ss), (vb, v_ss)):
        for ph in range(3):
            for i in range(3):
                sent(b[3 + ph], ss.at[ph * 3 + i])


def fused(stream, gain, w_gate, w_up, w_query, w_keyval, k_cache, v_cache, lengths):
    vm, dma = pltpu.VMEM, pltpu.SemaphoreType.DMA

    def rs(lead, wide, kind):
        ms = (16, 48, 16)
        return [
            *[vm(lead + (4, m, wide), kind) for m in ms],
            *[vm(lead + (m, wide), kind) for m in ms],
            *[vm(lead[:-1] + (2,) + lead[-1:] + (m, wide), kind) for m in ms],
        ]

    return pl.pallas_call(
        kernel,
        out_shape=(
            vm((16, FF), BF16),
            vm((2, HEADS * DH), BF16),
        ),
        in_specs=[pl.BlockSpec(memory_space=pl.ANY)] * 9,
        out_specs=[pl.BlockSpec(memory_space=pltpu.VMEM)] * 2,
        scratch_shapes=[
            vm((2, D), BF16), vm((1, D), F32), vm((T, 2, K, W), BF16),
            vm((K, 768), BF16), vm((64, K), BF16), vm((2, CACHE, DH), BF16), vm((2, CACHE, DH), BF16),
            pltpu.SMEM((2,), jnp.int32), dma((7,)), dma((T // 2,)),
            vm((4, 2, 4 * K), BF16), vm((4, 2, 4 * K), BF16), vm((4, 4, 2, K), BF16), vm((4, 8, K), F32),
            vm((8, 4, 8, K), BF16), vm((2, 64, 64), BF16), vm((2, 192, 192), BF16),
            vm((2, 64, K), BF16), vm((2, 192, K), BF16), vm((4, 16, W), F32),
            dma((3,)), dma((6,)),
            *rs((T, 2), W, BF16), *rs((3,), DH, F32), *rs((1,), 128, F32),
            dma((9,)), dma((T // 2, 6)), dma((9,)), dma((6,)), dma((9,)), dma((6,)),
            vm((8, 2, 896), BF16), vm((8, 2, 896), BF16), vm((2, HEADS, DH), F32), vm((16, 128), F32),
            dma((1,)), dma((1,)),
        ],
        compiler_params=pltpu.CompilerParams(
            collective_id=0, has_side_effects=True, vmem_limit_bytes=62 * 2**20
        ),
    )(stream, gain, w_gate, w_up, w_query, w_keyval, k_cache, v_cache, lengths)


def body(stream, norm_gain, w_gate, w_up, w_query, w_keyval, k_cache, v_cache, lengths):
    hidden, context = fused(
        stream, norm_gain.reshape(1, D), w_gate, w_up, w_query, w_keyval.T, k_cache, v_cache, lengths
    )
    return (hidden, context)


def solution(mesh):
    return jax.shard_map(
        body,
        mesh=mesh,
        in_specs=(
            P(("gx", "gy"), None),
            P(),
            P("gx", "gy"),
            P("gx", "gy"),
            P("gx", "gy"),
            P("gx", "gy"),
            P(("gx", "gy"), None, None),
            P(("gx", "gy"), None, None),
            P(("gx", "gy")),
        ),
        out_specs=(P("gx", "gy"), P(("gx", "gy"), None)),
        check_vma=False,
    )
```

time: 59.3 us -> 53.6 us (0.904)
  Pallas kernels: 57.3 us -> 51.3 us
    pallas_call x1, Pallas kernels: 57.3 us -> 51.3 us  [fused(): pl.pallas_call(kernel, out_shape=(vm((16, FF), BF16), vm((2, HEADS * DH),...]
where the time goes in v4:
time: 53.6 us; the launch traced here: 53.2 us
  Pallas kernels  51.3 us (96%)
  local copies, waits for them, and re-layouts  1.27 us (2%)
  between operations  0.64 us (1%)
    pallas_call x1, Pallas kernels, fused(): pl.pallas_call(kernel, out_shape=(vm((16, FF), BF16), vm((2, HEADS * DH),...  51.3 us
    unnamed x2, local copies, waits for them, and re-layouts  1.27 us

profile of v4, /device:TPU:1, one launch (start us, length us, event | category | flops | bytes accessed | tf_op | source)
XLA Modules:
  0.0 53.2 jit_solution(10409996445186148941)
XLA Ops:
  0.6 51.3 %shard_map.104 = (bf16[16,4608]{1,0:T(8,128)(2,1)S(1)}, bf16[2,6144]{1,0:T(2,128)(2,1)S(1)}) custom-call(bf16[2,18432]{1,0:T(2,128)(2,1)} %stream_h.1, f32[1,18432]{1,0:T(1,128)} %bitcast.3, bf16[1152,4608]{1,0:T(8,128)(2,1)} %wg_h.1, bf16[1152,4608]{1,0:T(8,128)(2,1)} %wu_h.1, bf16[1152,768]{1,0:T(8,128)(2,1)} %wq_h.1, bf16[64,1152]{1,0:T(8,128)(2,1)} %bitcast.2, ...), custom_call_target="tpu_custom_call" | custom-call | tf_op jit(solution)/shard_map/pallas_call | solution.py:403
  52.0 0.7 %copy.13 = bf16[16,4608]{1,0:T(8,128)(2,1)} copy(bf16[16,4608]{1,0:T(8,128)(2,1)S(1)} %get-tuple-element.2) | data formatting | bytes 294912
  52.6 0.6 %copy.14 = bf16[2,6144]{1,0:T(2,128)(2,1)} copy(bf16[2,6144]{1,0:T(2,128)(2,1)S(1)} %get-tuple-element.3) | data formatting | bytes 49152

commit v5 on v4

--- a/solution.py
+++ b/solution.py
@@ -95,7 +95,7 @@
     stream_h, gain_h, wg_h, wu_h, wq_h, wkv_h, k_h, v_h, lengths_h,
     hidden, context,
     stream, gain, wgu, wq, wkv, kc, vc, lengths, load_sem, wsem,
-    nsend, ybuf, zbuf, a8, xr, perm0, perm1, xs0, xs1, tmp,
+    nsend, ybuf, zbuf, a8, xr, perm0, perm1, xs0, xs1, tmp, both, join,
     d_ss, d_rs,
     *rest,
 ):
@@ -103,34 +103,19 @@
     f_ss, f_rs, q_ss, q_rs, v_ss, v_rs, qs, qr, qa, kvs, g_ss, g_rs = rest[27:]
     perm, xs = (perm0, perm1), (xs0, xs1)
     h = Place()
+    loads = [
+        pltpu.make_async_copy(src, dst, load_sem.at[i])
+        for i, (src, dst) in enumerate([(stream_h, stream), (gain_h, gain), (wq_h, wq), (wkv_h, wkv), (k_h, kc), (v_h, vc), (lengths_h, lengths)])
+    ]
+    for c in loads[:2]:
+        c.start()
+
     bar = pltpu.get_barrier_semaphore()
     for ax in "yz":
         for k in (1, 2, 3):
             pl.semaphore_signal(bar, inc=1, device_id=h.dev(ax, k), device_id_type=MESH)
     for k in range(1, 8):
         pl.semaphore_signal(bar, inc=1, device_id=(h.gx, lax.rem(h.gy + k, 8)), device_id_type=MESH)
-
-    loads = [
-        pltpu.make_async_copy(src, dst, load_sem.at[i])
-        for i, (src, dst) in enumerate([(stream_h, stream), (gain_h, gain), (wq_h, wq), (wkv_h, wkv), (k_h, kc), (v_h, vc), (lengths_h, lengths)])
-    ]
-    for c in loads[:4]:
-        c.start()
-
-    def wload(t):
-        cols = pl.ds(pl.multiple_of(t * W, 128), W)
-        return (
-            pltpu.make_async_copy(wg_h.at[:, cols], wgu.at[t, 0], wsem.at[t // 2]),
-            pltpu.make_async_copy(wu_h.at[:, cols], wgu.at[t, 1], wsem.at[t // 2]),
-        )
-
-    @pl.loop(0, T)
-    def _(t):
-        for c in wload(t):
-            c.start()
-
-    for c in loads[4:]:
-        c.start()
 
     loads[0].wait()
     loads[1].wait()
@@ -147,6 +132,43 @@
         v = (f32(stream[:, q * K:(q + 1) * K]) - mean) / root * gain[:, q * K:(q + 1) * K]
         nsend[q // 4, :, (q % 4) * K:(q % 4 + 1) * K] = v.astype(BF16)
 
+    pl.semaphore_wait(bar, 13)
+
+    def take(ref, sem):
+        pltpu.make_async_remote_copy(
+            ref, ref, sem, sem, device_id=h.dev("y", 1), device_id_type=MESH).wait_recv()
+
+    def sent(ref, sem):
+        pltpu.make_async_remote_copy(
+            ref, ref, sem, sem, device_id=h.dev("y", 1), device_id_type=MESH).wait_send()
+
+    first = [
+        pltpu.make_async_remote_copy(
+            nsend.at[h.at("y", k)], ybuf.at[h.y], d_ss.at[0], d_rs.at[0],
+            device_id=h.dev("y", k), device_id_type=MESH)
+        for k in (2, 1, 3)
+    ]
+    for c in first:
+        c.start()
+    ybuf[h.y] = nsend[h.y]
+    for c in loads[2:4]:
+        c.start()
+
+    def wload(t):
+        cols = pl.ds(pl.multiple_of(t * W, 128), W)
+        return (
+            pltpu.make_async_copy(wg_h.at[:, cols], wgu.at[t, 0], wsem.at[t // 2]),
+            pltpu.make_async_copy(wu_h.at[:, cols], wgu.at[t, 1], wsem.at[t // 2]),
+        )
+
+    @pl.loop(0, T)
+    def _(t):
+        for c in wload(t):
+            c.start()
+
+    for c in loads[4:]:
+        c.start()
+
     for part, m in ((0, 4), (1, 12)):
         i = lax.broadcasted_iota(jnp.int32, (16 * m, 16 * m), 0)
         j = lax.broadcasted_iota(jnp.int32, (16 * m, 16 * m), 1)
@@ -154,28 +176,13 @@
         rest_of = (j >> 6) * 4 + ((j >> 5) & 1) * 2 + (j & 1)
         for order, (u, v) in enumerate(((y, z), (z, y))):
             perm[part][order] = jnp.where(i == u * (4 * m) + v * m + rest_of, 1.0, 0.0).astype(BF16)
+    i = lax.broadcasted_iota(jnp.int32, (64, 64), 0)
+    j = lax.broadcasted_iota(jnp.int32, (64, 64), 1)
+    k, q = i >> 4, i & 15
+    join[...] = jnp.where(j == jnp.where(q < 4, k * 4 + q, 12 + k * 12 + q), 1.0, 0.0).astype(BF16)
     vb[0][...] = jnp.zeros_like(vb[0])
     vb[1][...] = jnp.zeros_like(vb[1])
 
-    pl.semaphore_wait(bar, 13)
-
-    def take(ref, sem):
-        pltpu.make_async_remote_copy(
-            ref, ref, sem, sem, device_id=h.dev("y", 1), device_id_type=MESH).wait_recv()
-
-    def sent(ref, sem):
-        pltpu.make_async_remote_copy(
-            ref, ref, sem, sem, device_id=h.dev("y", 1), device_id_type=MESH).wait_send()
-
-    first = [
-        pltpu.make_async_remote_copy(
-            nsend.at[h.at("y", k)], ybuf.at[h.y], d_ss.at[0], d_rs.at[0],
-            device_id=h.dev("y", k), device_id_type=MESH)
-        for k in (2, 1, 3)
-    ]
-    for c in first:
-        c.start()
-    ybuf[h.y] = nsend[h.y]
     take(ybuf.at[0:3], d_rs.at[0])
 
     def zcols(zd):
@@ -260,8 +267,8 @@
         @pl.loop(lo, hi)
         def _(i):
             if part == 0:
-                both = wgu.at[pl.ds(2 * i, 2)]
-                pltpu.make_async_copy(both, both, wsem.at[i]).wait()
+                blocks = wgu.at[pl.ds(2 * i, 2)]
+                pltpu.make_async_copy(blocks, blocks, wsem.at[i]).wait()
             for order in (0, 1):
                 t = 2 * i + order
                 for n in (0, 1):
@@ -280,7 +287,17 @@
         def _(i):
             for ph in (0, 1):
                 pair_take(i, ph, 1)
-            pair(i, lambda t, ss: [s.turn(direct) for s in ss])
+            group = []
+            pair(i, lambda t, ss: group.extend(ss))
+            for n, s in enumerate(group):
+                cols = slice(n * W, (n + 1) * W)
+                both[0:16, cols] = s.total(0).astype(BF16)
+                both[16:64, cols] = s.total(1).astype(BF16)
+            for n, s in enumerate(group):
+                val = jnp.dot(join[...], both[:, n * W:(n + 1) * W], preferred_element_type=F32)
+                s.mid[...] = val.astype(BF16).reshape(4, 16, W)
+            for s in group:
+                s.start(2, direct)
 
     def att_relay(ph):
         att_take(ph, 0)
@@ -291,14 +308,13 @@
     loads[2].wait()
     loads[3].wait()
     query(0)
-    computes(0, 0, 4)
-    att_relay(0)
-    relays(0, 0, 2)
-    computes(0, 4, T // 2)
+    computes(0, 0, T // 2)
     rows(1)
     query(1)
+    att_relay(0)
+    relays(0, 0, 4)
     computes(1, 0, 2)
-    relays(0, 2, T // 2)
+    relays(0, 4, T // 2)
     computes(1, 2, 4)
     att_relay(1)
     computes(1, 4, T // 2)
@@ -309,7 +325,6 @@
         s.turn(True)
     relays(1, 3, T // 2)
     turns(0, DIRECT, False)
-    turns(DIRECT, T // 2, True)
 
     att_take(2, 0)
     att_take(2, 1)
@@ -326,6 +341,8 @@
     for c in give:
         c.start()
     qr[h.gy] = qs[h.c]
+    turns(DIRECT, T // 2, True)
+
     relays(2, 0, DIRECT)
 
     take(qr.at[0:7], g_rs.at[0])
@@ -415,6 +432,7 @@
             vm((4, 2, 4 * K), BF16), vm((4, 2, 4 * K), BF16), vm((4, 4, 2, K), BF16), vm((4, 8, K), F32),
             vm((8, 4, 8, K), BF16), vm((2, 64, 64), BF16), vm((2, 192, 192), BF16),
             vm((2, 64, K), BF16), vm((2, 192, K), BF16), vm((4, 16, W), F32),
+            vm((64, 4 * W), BF16), vm((64, 64), BF16),
             dma((3,)), dma((6,)),
             *rs((T, 2), W, BF16), *rs((3,), DH, F32), *rs((1,), 128, F32),
             dma((9,)), dma((T // 2, 6)), dma((9,)), dma((6,)), dma((9,)), dma((6,)),
@@ -427,11 +445,31 @@
     )(stream, gain, w_gate, w_up, w_query, w_keyval, k_cache, v_cache, lengths)
 
 
+def write(hidden, context, hidden_h, context_h, sem):
+    copies = [
+        pltpu.make_async_copy(hidden, hidden_h, sem.at[0]),
+        pltpu.make_async_copy(context, context_h, sem.at[1]),
+    ]
+    for c in copies:
+        c.start()
+    for c in copies:
+        c.wait()
+
+
 def body(stream, norm_gain, w_gate, w_up, w_query, w_keyval, k_cache, v_cache, lengths):
     hidden, context = fused(
         stream, norm_gain.reshape(1, D), w_gate, w_up, w_query, w_keyval.T, k_cache, v_cache, lengths
     )
-    return (hidden, context)
+    return pl.pallas_call(
+        write,
+        out_shape=(
+            jax.ShapeDtypeStruct((16, FF), BF16),
+            jax.ShapeDtypeStruct((2, HEADS * DH), BF16),
+        ),
+        in_specs=[pl.BlockSpec(memory_space=pl.ANY)] * 2,
+        out_specs=[pl.BlockSpec(memory_space=pl.ANY)] * 2,
+        scratch_shapes=[pltpu.SemaphoreType.DMA((2,))],
+    )(*(pltpu.with_memory_space_constraint(v, pltpu.VMEM) for v in (hidden, context)))
 
 
 def solution(mesh):

time: 53.6 us -> 52.4 us (0.978)
  local copies, waits for them, and re-layouts: 1.27 us -> 0 us
    unnamed x2 -> x0, local copies, waits for them, and re-layouts: 1.27 us -> none
    pallas_call x0 -> x1, Pallas kernels: none -> 0.68 us  [body(): pl.pallas_call(write, out_shape=(jax.ShapeDtypeStruct((16, FF), BF16), ja...]
where the time goes in v5:
time: 52.4 us; the launch traced here: 52.2 us
  Pallas kernels  51.6 us (98%)
  between operations  0.64 us (1%)
    pallas_call x1, Pallas kernels, fused(): pl.pallas_call(kernel, out_shape=(vm((16, FF), BF16), vm((2, HEADS * DH),...  50.9 us

profile of v5, /device:TPU:1, one launch (start us, length us, event | category | flops | bytes accessed | tf_op | source)
XLA Modules:
  0.0 52.2 jit_solution(14633891675988062196)
XLA Ops:
  0.6 50.9 %shard_map.104 = (bf16[16,4608]{1,0:T(8,128)(2,1)S(1)}, bf16[2,6144]{1,0:T(2,128)(2,1)S(1)}) custom-call(bf16[2,18432]{1,0:T(2,128)(2,1)} %stream_h.1, f32[1,18432]{1,0:T(1,128)} %bitcast.3, bf16[1152,4608]{1,0:T(8,128)(2,1)} %wg_h.1, bf16[1152,4608]{1,0:T(8,128)(2,1)} %wu_h.1, bf16[1152,768]{1,0:T(8,128)(2,1)} %wq_h.1, bf16[64,1152]{1,0:T(8,128)(2,1)} %bitcast.2, ...), custom_call_target="tpu_custom_call" | custom-call | tf_op jit(solution)/shard_map/pallas_call | solution.py:420
  51.6 0.7 %shard_map.105 = (bf16[16,4608]{1,0:T(8,128)(2,1)}, bf16[2,6144]{1,0:T(2,128)(2,1)}) custom-call(bf16[16,4608]{1,0:T(8,128)(2,1)S(1)} %get-tuple-element.4.hidden, bf16[2,6144]{1,0:T(2,128)(2,1)S(1)} %get-tuple-element.5.context), custom_call_target="tpu_custom_call" | custom-call | tf_op jit(solution)/shard_map/pallas_call | solution.py:463

commit v6 on v5

--- a/solution.py
+++ b/solution.py
@@ -319,12 +319,14 @@
     att_relay(1)
     computes(1, 4, T // 2)
     relays(1, 0, 3)
+    relays(1, 3, T // 2)
     for ph in (0, 1):
         att_take(ph, 1)
     for s in att:
         s.turn(True)
-    relays(1, 3, T // 2)
     turns(0, DIRECT, False)
+
+    turns(DIRECT, T // 2, True)
 
     att_take(2, 0)
     att_take(2, 1)
@@ -341,8 +343,6 @@
     for c in give:
         c.start()
     qr[h.gy] = qs[h.c]
-    turns(DIRECT, T // 2, True)
-
     relays(2, 0, DIRECT)
 
     take(qr.at[0:7], g_rs.at[0])

time: 52.4 us -> 52.2 us (level)
  no operation moved by 1% of the time
where the time goes in v6:
time: 52.2 us; the launch traced here: 52.1 us
  Pallas kernels  51.4 us (98%)
  between operations  0.64 us (1%)
    pallas_call x1, Pallas kernels, fused(): pl.pallas_call(kernel, out_shape=(vm((16, FF), BF16), vm((2, HEADS * DH),...  50.8 us

profile of v6, /device:TPU:1, one launch (start us, length us, event | category | flops | bytes accessed | tf_op | source)
XLA Modules:
  0.0 52.1 jit_solution(2526288196492851154)
XLA Ops:
  0.6 50.8 %shard_map.104 = (bf16[16,4608]{1,0:T(8,128)(2,1)S(1)}, bf16[2,6144]{1,0:T(2,128)(2,1)S(1)}) custom-call(bf16[2,18432]{1,0:T(2,128)(2,1)} %stream_h.1, f32[1,18432]{1,0:T(1,128)} %bitcast.3, bf16[1152,4608]{1,0:T(8,128)(2,1)} %wg_h.1, bf16[1152,4608]{1,0:T(8,128)(2,1)} %wu_h.1, bf16[1152,768]{1,0:T(8,128)(2,1)} %wq_h.1, bf16[64,1152]{1,0:T(8,128)(2,1)} %bitcast.2, ...), custom_call_target="tpu_custom_call" | custom-call | tf_op jit(solution)/shard_map/pallas_call | solution.py:420
  51.4 0.7 %shard_map.105 = (bf16[16,4608]{1,0:T(8,128)(2,1)}, bf16[2,6144]{1,0:T(2,128)(2,1)}) custom-call(bf16[16,4608]{1,0:T(8,128)(2,1)S(1)} %get-tuple-element.4.hidden, bf16[2,6144]{1,0:T(2,128)(2,1)S(1)} %get-tuple-element.5.context), custom_call_target="tpu_custom_call" | custom-call | tf_op jit(solution)/shard_map/pallas_call | solution.py:463
